TPU v7x, 32 devices: a whole 2x2x4 slice. The times are simulated.
32 devices in a mesh: img: 4 (over z), tile: 8 (over y, x, core).
Axes of the slice: x: 2, y: 2, z: 4, core: 2. Of those that a mesh axis runs over, the one named last changes fastest.
Arguments:
- features: bfloat16 [64, 2400, 256], P(('img', 'tile')), may hold values from -6 to 6
- cluster_ids: int32 [64, 4, 2400], P(('img', 'tile')), may hold values from 0 to 63
- soft_weights: bfloat16 [64, 4, 2400], P(('img', 'tile')), may hold values from 0.019897461 to 1
- counts: int32 [64], P(('img', 'tile')), may hold values from 600 to 2400, as said below
- centroids: bfloat16 [64, 256], replicated, may hold values from -3 to 3
- covariance: float32 [16384, 16384], P('img', 'tile'), may hold values from -1.5 to 1.5
Outputs:
- updated: float32 [16384, 16384], P('img', 'tile')
Inputs may be any that keep to these rules, and one draw needn't show every extreme that they name: `counts`: some image has exactly 2400 valid features and some exactly 600.
All inputs are finite; a program needn't handle non-finite values.
Results may differ from a plain program's by a relative error of at most 0.0003.
Values sent between devices are 32-bit elements; how exact they have to be, the bound alone decides.
No kernel may reach another device: no remote copies, remote signals or barrier semaphores. Data moves between devices by JAX's collectives and lax.ppermute only.
A program may use at most 128 MiB of HBM per device.

v0:
```python
import jax
import jax.numpy as jnp
from jax import lax
from jax.sharding import PartitionSpec as P


def aggregate(features, cluster_ids, soft_weights, counts, centroids):
    img_dev, top_count, max_slots = cluster_ids.shape
    cluster_count = centroids.shape[0]
    labels = lax.broadcasted_iota(jnp.int32, (1, cluster_count, 1), 1)
    assign = jnp.zeros((img_dev, cluster_count, max_slots), jnp.float32)
    for slot in range(top_count):
        matched = cluster_ids[:, slot : slot + 1, :] == labels
        assign = assign + jnp.where(
            matched, soft_weights[:, slot : slot + 1, :].astype(jnp.float32), 0.0
        )
    in_range = lax.broadcasted_iota(jnp.int32, (1, 1, max_slots), 2) < counts[:, None, None]
    assign = jnp.where(in_range, assign, 0.0).astype(jnp.bfloat16)
    weight_sum = jnp.sum(assign, axis=2, dtype=jnp.float32)
    residual = jnp.einsum("ikf,ifc->ikc", assign, features, preferred_element_type=jnp.float32)
    residual = residual - weight_sum[:, :, None] * centroids.astype(jnp.float32)[None, :, :]
    magnitude = jnp.sqrt(jnp.sum(residual * residual, axis=2, keepdims=True) + 1e-06)
    return (residual / magnitude).reshape(img_dev, -1)


def outer_block(left_rows, right_rows):
    return lax.dot_general(
        left_rows,
        right_rows,
        (((0,), (0,)), ((), ())),
        precision=lax.Precision.HIGHEST,
        preferred_element_type=jnp.float32,
    )


def body(features, cluster_ids, soft_weights, counts, centroids, covariance):
    vlad_rows = aggregate(features, cluster_ids, soft_weights, counts, centroids)
    img_shards = lax.axis_size("img")
    tile_shards = lax.axis_size("tile")
    img_dev = vlad_rows.shape[0]
    width_rows = covariance.shape[0]
    width_cols = covariance.shape[1]
    factor = float(centroids.shape[1]) / float(img_dev * img_shards * tile_shards)
    row_part = vlad_rows.reshape(img_dev, img_shards, 1, width_rows).transpose(1, 2, 0, 3)
    row_part = jnp.broadcast_to(row_part, (img_shards, tile_shards, img_dev, width_rows))
    col_part = vlad_rows.reshape(img_dev, 1, tile_shards, width_cols).transpose(1, 2, 0, 3)
    col_part = jnp.broadcast_to(col_part, (img_shards, tile_shards, img_dev, width_cols))
    outgoing = jnp.concatenate((row_part, col_part), axis=3)
    outgoing = outgoing.reshape(img_shards * tile_shards * img_dev, width_rows + width_cols)
    incoming = lax.all_to_all(outgoing, ("img", "tile"), split_axis=0, concat_axis=0, tiled=True)
    product = outer_block(incoming[:, :width_rows], incoming[:, width_rows:])
    return covariance + factor * product


def solution(mesh):
    return jax.shard_map(
        body,
        mesh=mesh,
        in_specs=(
            P(("img", "tile"), None, None),
            P(("img", "tile"), None, None),
            P(("img", "tile"), None, None),
            P(("img", "tile")),
            P(),
            P("img", "tile"),
        ),
        out_specs=P("img", "tile"),
        check_vma=False,
    )
```

profile of v0, /device:TPU:0, one launch (start us, length us, event | category | flops | bytes accessed | tf_op | source)
XLA Modules:
  0.0 91.3 jit_solution(7759167873453074827)
XLA Ops:
  0.0 0.0 copy-start
  0.0 0.9 iota_compare_fusion.4
  0.9 0.8 convert_element_type.15
  1.7 1.2 %fusion.3 = (s32[2,1,2400]{2,1,0:T(1,128)S(1)}, s32[2,1,2400]{2,1,0:T(1,128)S(1)}, s32[2,1,2400]{2,1,0:T(1,128)S(1)}, s32[2,1,2400]{2,1,0:T(1,128)S(1)}) fusion(s32[2,4,2400]{2,1,0:T(4,128)} %param.7), kind=kLoop, calls=%fused_computation.28 | loop fusion | bytes 153600 | tf_op jit(solution)/shard_map/slice | solution.py:13
  2.8 1.0 %slice_convert_fusion.3 = (f32[2,1,2400]{2,1,0:T(1,128)S(1)}, f32[2,1,2400]{2,1,0:T(1,128)S(1)}, f32[2,1,2400]{2,1,0:T(1,128)S(1)}, f32[2,1,2400]{2,1,0:T(1,128)S(1)}) fusion(bf16[2,4,2400]{2,1,0:T(4,128)(2,1)} %param.8), kind=kLoop, calls=%fused_computation.24 | loop fusion | flops 19200 | bytes 115200 | tf_op jit(solution)/shard_map/jit(_where)/broadcast_in_dim | solution.py:14
  3.9 1.0 %convert_reduce_fusion = f32[2,64]{1,0:T(2,128)S(1)} fusion(f32[2,2400]{1,0:T(2,128)S(1)} %get-tuple-element.15, s32[2,2400]{1,0:T(2,128)S(1)} %get-tuple-element.19, f32[2,2400]{1,0:T(2,128)S(1)} %get-tuple-element.16, s32[2,2400]{1,0:T(2,128)S(1)} %get-tuple-element.20, f32[2,2400]{1,0:T(2,128)S(1)} %get-tuple-element.17, ...), kind=kLoop, calls=%fused_computation.2 | loop fusion | flops 4607872 | bytes 158912 | tf_op jit(solution)/shard_map/reduce_sum | solution.py:19
  5.0 0.0 copy-done
  5.0 1.0 %multiply_reduce_fusion = (f32[2,64]{1,0:T(2,128)S(1)}, f32[2,64,256]{2,1,0:T(8,128)S(1)}) fusion(f32[64,256]{1,0:T(8,128)S(1)} %convert_element_type.15, f32[2,64]{1,0:T(2,128)S(1)} %convert_reduce_fusion, bf16[2,2400,256]{2,1,0:T(8,128)(2,1)S(1)} %copy-done, f32[2,2400]{1,0:T(2,128)S(1)} %get-tuple-element.15, s32[2,2400]{1,0:T(2,128)S(1)} %get-tuple-element.19, ...), kind=kOutput, calls=%fused_computation.11 | convolution fusion | flops 161410944 | bytes 2813632 | tf_op jit(solution)/shard_map/ikf,ifc->ikc/dot_general | solution.py:20
  6.0 0.1 broadcast_divide_fusion
  6.1 0.1 reshape_reshape.6
  6.2 0.1 copy.9
  6.3 0.1 copy.10
  6.4 0.2 broadcast_in_dim.95
  6.7 0.5 broadcast_in_dim.93
  7.1 0.7 pad_maximum_fusion
  7.9 45.3 %all_to_all.12 = f32[32,2,6144]{2,1,0:T(2,128)} all-to-all(f32[32,2,6144]{2,1,0:T(2,128)S(1)} %bitcast.24), channel_id=1, replica_groups=mesh['img'=4,'tile'=8] {'img','tile'}, dimensions={0} | all-to-all | bytes 3145728 | tf_op jit(solution)/shard_map/all_to_all | solution.py:50
  53.2 3.2 %all_to_all.10 = f32[64,6144]{1,0:T(8,128)} reshape(f32[32,2,6144]{2,1,0:T(2,128)} %all_to_all.12) | data formatting | bytes 3145728 | tf_op jit(solution)/shard_map/all_to_all | solution.py:50
  56.4 0.0 copy-start.1
  56.4 34.9 %multiply_add_fusion = f32[4096,2048]{1,0:T(8,128)} fusion(f32[4096,2048]{1,0:T(8,128)} %param.11, f32[64,6144]{1,0:T(8,128)} %all_to_all.10), kind=kOutput, calls=%fused_computation | convolution fusion | flops 6459228160 | bytes 68681728 | tf_op jit(solution)/shard_map/dot_general | solution.py:27
  91.3 0.0 copy-done.1
  (6 shorter events, 0.1 us)
Async XLA Ops:
  0.0 5.0 %copy-start = (bf16[2,2400,256]{2,1,0:T(8,128)(2,1)S(1)}, bf16[2,2400,256]{2,1,0:T(8,128)(2,1)}, u32[]{:S(2)}) copy-start(bf16[2,2400,256]{2,1,0:T(8,128)(2,1)} %param.6) | copy-start | bytes 7372804
  56.4 34.9 %copy-start.1 = (bf16[2,2400,256]{2,1,0:T(8,128)(2,1)S(1)}, bf16[2,2400,256]{2,1,0:T(8,128)(2,1)}, u32[]{:S(2)}) copy-start(bf16[2,2400,256]{2,1,0:T(8,128)(2,1)} %param.6) | copy-start | bytes 7372804
where the time goes:
time: 91.6 us; the launch traced here: 91.3 us
  blocking collectives  45.3 us (49%)
  matrix products  35.9 us (39%)
  local copies, waits for them, and re-layouts  5.49 us (6%)
  other arithmetic  4.51 us (5%)
    all_to_all x1, blocking collectives, body(): lax.all_to_all(outgoing, ('img', 'tile'), split_axis=0, concat_axis=0, ti...  45.3 us
    dot_general x1, matrix products, outer_block(): lax.dot_general(left_rows, right_rows, (((0,), (0,)), ((), ())), precisio...  34.9 us
    all_to_all x1, local copies, waits for them, and re-layouts, body(): lax.all_to_all(outgoing, ('img', 'tile'), split_axis=0, concat_axis=0, ti...  3.25 us

commit v1 on v0

v1 whole, which is shorter than its diff:
```python
import functools

import jax
import jax.numpy as jnp
from jax import lax
from jax.experimental import pallas as pl
from jax.experimental.pallas import tpu as pltpu
from jax.sharding import PartitionSpec as P

VMEM = pltpu.VMEM
BF16 = jnp.bfloat16
F32 = jnp.float32


def aggregate_kernel(counts, ids, weights, centroids, features, rows):
    image = pl.program_id(0)
    top, slots = ids.shape[1:]
    clusters = centroids.shape[0]
    position = lax.broadcasted_iota(jnp.int32, (top, slots), 1)
    valid_ids = jnp.where(position < counts[image], ids[0], -1)
    values = weights[0].astype(F32)
    labels = lax.broadcasted_iota(jnp.int32, (clusters, slots), 0)
    assign = jnp.zeros((clusters, slots), F32)
    for slot in range(top):
        matched = valid_ids[slot : slot + 1] == labels
        assign = assign + jnp.where(matched, values[slot : slot + 1], 0.0)
    assign = assign.astype(BF16)
    weight_sum = jnp.sum(assign.astype(F32), axis=1, keepdims=True)
    residual = jnp.dot(assign, features[0], preferred_element_type=F32)
    residual = residual - weight_sum * centroids[...].astype(F32)
    square = jnp.sum(residual * residual, axis=1, keepdims=True)
    rows[0] = residual / jnp.sqrt(square + 1e-06)


def aggregate(features, cluster_ids, soft_weights, counts, centroids):
    images, slots, width = features.shape
    top = cluster_ids.shape[1]
    clusters = centroids.shape[0]
    return pl.pallas_call(
        aggregate_kernel,
        grid=(images,),
        in_specs=[
            pl.BlockSpec(memory_space=pltpu.SMEM),
            pl.BlockSpec((1, top, slots), lambda i: (i, 0, 0)),
            pl.BlockSpec((1, top, slots), lambda i: (i, 0, 0)),
            pl.BlockSpec((clusters, width), lambda i: (0, 0)),
            pl.BlockSpec((1, slots, width), lambda i: (i, 0, 0)),
        ],
        out_specs=pl.BlockSpec((1, clusters, width), lambda i: (i, 0, 0)),
        out_shape=jax.ShapeDtypeStruct((images, clusters, width), F32),
        compiler_params=pltpu.CompilerParams(vmem_limit_bytes=16 << 20),
        name="aggregate",
    )(counts, cluster_ids, soft_weights, centroids, features)


def pack_kernel(peers, block, own, other, *parts):
    core = lax.rem(lax.axis_index("tile"), 2)
    me = jnp.where(core == 0, lax.axis_index("img"), lax.axis_index("tile") // 2)
    images = own.shape[0]
    for step in range(peers):
        start = pl.multiple_of(lax.bitwise_xor(me, step) * block, block)
        parts[step][pl.ds(core * images, images)] = own[:, pl.ds(start, block)]
        parts[step][pl.ds((1 - core) * images, images)] = other[:, pl.ds(start, block)]


def pack(own, other, peers, block):
    images, _, width = own.shape
    return pl.pallas_call(
        functools.partial(pack_kernel, peers, block),
        in_specs=[pl.BlockSpec(memory_space=VMEM)] * 2,
        out_specs=[pl.BlockSpec(memory_space=VMEM)] * peers,
        out_shape=[jax.ShapeDtypeStruct((2 * images, block, width), F32)] * peers,
        compiler_params=pltpu.CompilerParams(vmem_limit_bytes=4 << 20),
        name="pack",
    )(own, other)


def load_kernel(block, source, target, sems):
    steps = source.shape[0] // block
    copies = [
        pltpu.make_async_copy(
            source.at[pl.ds(i * block, block)], target.at[pl.ds(i * block, block)], sems.at[i]
        )
        for i in range(steps)
    ]
    for copy in copies:
        copy.start()
    for copy in copies:
        copy.wait()


def load(covariance, block):
    rows, cols = covariance.shape
    size = rows * cols * 4
    return pl.pallas_call(
        functools.partial(load_kernel, block),
        in_specs=[pl.BlockSpec(memory_space=pl.ANY)],
        out_specs=pl.BlockSpec(memory_space=VMEM),
        out_shape=VMEM((rows, cols), F32),
        scratch_shapes=[pltpu.SemaphoreType.DMA((rows // block,))],
        compiler_params=pltpu.CompilerParams(vmem_limit_bytes=1 << 20),
        cost_estimate=pl.CostEstimate(flops=0, bytes_accessed=size, transcendentals=0),
        name="load",
    )(covariance)


def split(value):
    high = value.astype(BF16)
    low = (value - high.astype(F32)).astype(BF16)
    return high, low


def update_kernel(peers, factor, stages, *refs):
    mine, theirs = refs[:peers], refs[peers : 2 * peers]
    covariance, updated, left, right, stage, sems = refs[2 * peers :]
    core = lax.rem(lax.axis_index("tile"), 2)
    group, block, width = mine[0].shape
    part = group // peers
    count = group * peers
    half = block // 2

    def prepare(row_refs, col_refs, base):
        for k in range(half):
            pieces = []
            for j in range(peers):
                for t in range(peers):
                    pieces.append(col_refs[t][j * part : (j + 1) * part, base + k, :])
            high, low = split(jnp.concatenate(pieces, axis=0) * factor)
            columns = slice(k * width, (k + 1) * width)
            right[0 * count : 1 * count, columns] = high
            right[1 * count : 2 * count, columns] = low
            right[2 * count : 3 * count, columns] = high
        for k in range(block):
            pieces = [row_refs[j][:, k, :] for j in range(peers)]
            high, low = split(jnp.concatenate(pieces, axis=0))
            left[k, 0 * count : 1 * count] = high
            left[k, 1 * count : 2 * count] = high
            left[k, 2 * count : 3 * count] = low

    @pl.when(core == 0)
    def _():
        prepare(mine, theirs, 0)

    @pl.when(core == 1)
    def _():
        prepare(theirs, mine, half)

    def copy_out(step, slot):
        start = pl.multiple_of(step * width, width)
        return pltpu.make_async_copy(stage.at[slot], updated.at[pl.ds(start, width)], sems.at[slot])

    def row_step(step, carry):
        slot = lax.rem(step, stages)

        @pl.when(step >= stages)
        def _():
            copy_out(step - stages, slot).wait()

        product = lax.dot_general(
            left[step], right[...], (((0,), (0,)), ((), ())), preferred_element_type=F32
        )
        start = pl.multiple_of(step * width, width)
        stage[slot] = covariance[pl.ds(start, width)] + product
        copy_out(step, slot).start()
        return carry

    lax.fori_loop(0, block, row_step, 0)
    for step in range(max(block - stages, 0), block):
        copy_out(step, step % stages).wait()


def update(mine, theirs, covariance, factor):
    peers = len(mine)
    group, block, width = mine[0].shape
    count = group * peers
    rows, cols = covariance.shape
    stages = 3
    return pl.pallas_call(
        functools.partial(update_kernel, peers, factor, stages),
        in_specs=[pl.BlockSpec(memory_space=VMEM)] * (2 * peers + 1),
        out_specs=pl.BlockSpec(memory_space=pl.ANY),
        out_shape=jax.ShapeDtypeStruct((rows, cols), F32),
        scratch_shapes=[
            VMEM((block, 3 * count, width), BF16),
            VMEM((3 * count, cols), BF16),
            VMEM((stages, width, cols), F32),
            pltpu.SemaphoreType.DMA((stages,)),
        ],
        compiler_params=pltpu.CompilerParams(vmem_limit_bytes=12 << 20),
        name="update",
    )(*mine, *theirs, covariance)


def body(features, cluster_ids, soft_weights, counts, centroids, covariance):
    peers = lax.axis_size("img")
    tiles = lax.axis_size("tile")
    clusters, width = centroids.shape
    images = features.shape[0]
    block = clusters // peers
    factor = float(width) / float(images * peers * tiles)

    def device(img, group, core):
        return (img * (tiles // 2) + group) * 2 + core

    everyone = [(i, g, c) for i in range(peers) for g in range(tiles // 2) for c in range(2)]

    def send(value, target):
        pairs = [(device(*d), device(*target(*d))) for d in everyone]
        return lax.ppermute(value, ("img", "tile"), pairs)

    def to_other(value):
        return send(value, lambda i, g, c: (i, g, 1 - c))

    def first(value, k):
        return send(value, lambda i, g, c: (i ^ k, g, c) if c == 0 else (i, g ^ k, c))

    def second(value, k):
        return send(value, lambda i, g, c: (i, g ^ k, c) if c == 0 else (i ^ k, g, c))

    own = aggregate(features, cluster_ids, soft_weights, counts, centroids)
    other = to_other(own)
    parts = pack(own, other, peers, block)
    received = [parts[0]]
    for k in range(1, peers):
        received.append(first(parts[k], k))
    gathered = jnp.concatenate(received, axis=0)
    mine = [gathered]
    for k in range(1, peers):
        mine.append(second(gathered, k))
    theirs = []
    for k in range(peers):
        theirs.append(to_other(mine[k]))
    held = load(covariance, 2 * width)
    return update(mine, theirs, held, factor)


def solution(mesh):
    return jax.shard_map(
        body,
        mesh=mesh,
        in_specs=(
            P(("img", "tile"), None, None),
            P(("img", "tile"), None, None),
            P(("img", "tile"), None, None),
            P(("img", "tile")),
            P(),
            P("img", "tile"),
        ),
        out_specs=P("img", "tile"),
        check_vma=False,
    )
```

time: 91.6 us -> 54.1 us (0.59)
  blocking collectives: 45.3 us -> 0 us
  matrix products: 35.9 us -> 0 us
  Pallas kernels: 0 us -> 24.6 us
  waiting for transfers between devices: 0 us -> 13.5 us
  starting transfers between devices: 0 us -> 10.7 us
  other arithmetic: 4.51 us -> 0 us
    all_to_all x1 -> x0, blocking collectives: 45.3 us -> none  [body(): lax.all_to_all(outgoing, ('img', 'tile'), split_axis=0, concat_axis=0, ti...]
    dot_general x2 -> x0, matrix products: 35.9 us -> none  [the longest x1 34.9 us: outer_block(): lax.dot_general(left_rows, right_rows, (((0,), (0,)), ((), ())), precisio...]
    pallas_call x0 -> x4, Pallas kernels: none -> 24.6 us  [the longest x1 12.2 us: update(): pl.pallas_call(functools.partial(update_kernel, peers, factor, stages), i...]
    ppermute x0 -> x11, waiting for transfers between devices: none -> 13.5 us  [send(): return lax.ppermute(value, ('img', 'tile'), pairs)]
    ppermute x0 -> x11, starting transfers between devices: none -> 10.7 us  [send(): return lax.ppermute(value, ('img', 'tile'), pairs)]
    unnamed x8 -> x13, local copies, waits for them, and re-layouts: 0.1 us -> 4.78 us
    all_to_all x1 -> x0, local copies, waits for them, and re-layouts: 3.25 us -> none  [body(): lax.all_to_all(outgoing, ('img', 'tile'), split_axis=0, concat_axis=0, ti...]
    slice x1 -> x0, local copies, waits for them, and re-layouts: 1.15 us -> none  [aggregate(): matched = cluster_ids[:, slot:slot + 1, :] == labels]
  transfers between devices with their start and end apart: 0 -> 11, of which waited for: 0 -> 5; matrix products, arithmetic and copies ran while one was open for 0% -> 0% of each run, Pallas kernels for 0% -> 20%
where the time goes in v1:
time: 54.1 us; the launch traced here: 53.8 us
  Pallas kernels  24.6 us (45%)
  waiting for transfers between devices  13.5 us (25%)
  starting transfers between devices  10.7 us (20%)
  local copies, waits for them, and re-layouts  4.79 us (9%)
    ppermute x11, waiting for transfers between devices, send(): return lax.ppermute(value, ('img', 'tile'), pairs)  13.5 us
    pallas_call x1, Pallas kernels, update(): pl.pallas_call(functools.partial(update_kernel, peers, factor, stages), i...  12.2 us
    ppermute x11, starting transfers between devices, send(): return lax.ppermute(value, ('img', 'tile'), pairs)  10.7 us
    pallas_call x1, Pallas kernels, load(): pl.pallas_call(functools.partial(load_kernel, block), in_specs=[pl.BlockS...  10.7 us
    unnamed x13, local copies, waits for them, and re-layouts  4.78 us
    pallas_call x1, Pallas kernels, aggregate(): pl.pallas_call(aggregate_kernel, grid=(images,), in_specs=[pl.BlockSpec(m...  1.73 us
  transfers between devices with their start and end apart: 11, of which 5 were waited for; matrix products, arithmetic and copies ran while one was open for 0% of the time, Pallas kernels for 20%

profile of v1, /device:TPU:0, one launch (start us, length us, event | category | flops | bytes accessed | tf_op | source)
XLA Modules:
  0.0 53.8 jit_solution(10657212878068166572)
XLA Ops:
  0.0 1.7 %copy-done = bf16[2,2400,256]{2,1,0:T(8,128)(2,1)S(1)} copy-done((bf16[2,2400,256]{2,1,0:T(8,128)(2,1)S(1)}, bf16[2,2400,256]{2,1,0:T(8,128)(2,1)}, u32[]{:S(2)}) %copy-start) | copy-done | bytes 2457624
  1.7 0.9 %copy-done.1 = s32[2,4,2400]{2,1,0:T(4,128)S(1)} copy-done((s32[2,4,2400]{2,1,0:T(4,128)S(1)}, s32[2,4,2400]{2,1,0:T(4,128)}, u32[]{:S(2)}) %copy-start.1) | copy-done | bytes 76824
  2.6 0.8 %copy-done.2 = bf16[2,4,2400]{2,1,0:T(4,128)(2,1)S(1)} copy-done((bf16[2,4,2400]{2,1,0:T(4,128)(2,1)S(1)}, bf16[2,4,2400]{2,1,0:T(4,128)(2,1)}, u32[]{:S(2)}) %copy-start.2) | copy-done | bytes 38424
  3.4 0.8 %copy-done.3 = bf16[64,256]{1,0:T(8,128)(2,1)S(1)} copy-done((bf16[64,256]{1,0:T(8,128)(2,1)S(1)}, bf16[64,256]{1,0:T(8,128)(2,1)}, u32[]{:S(2)}) %copy-start.3) | copy-done | bytes 32792
  4.1 0.7 %copy-done.4 = s32[2]{0:T(128)S(1)} copy-done((s32[2]{0:T(128)S(1)}, s32[2]{0:T(128)}, u32[]{:S(2)}) %copy-start.4) | copy-done | bytes 32
  4.8 1.7 %aggregate.1.own = f32[2,64,256]{2,1,0:T(8,128)S(1)} custom-call(s32[2]{0:T(128)S(1)} %copy-done.4, s32[2,4,2400]{2,1,0:T(4,128)S(1)} %copy-done.1, bf16[2,4,2400]{2,1,0:T(4,128)(2,1)S(1)} %copy-done.2, bf16[64,256]{1,0:T(8,128)(2,1)S(1)} %copy-done.3, bf16[2,2400,256]{2,1,0:T(8,128)(2,1)S(1)} %copy-done), custom_call_target="tpu_custom_call" | custom-call | tf_op jit(solution)/shard_map/aggregate/pallas_call | solution.py:39
  6.5 0.6 %collective-permute-start = (f32[2,64,256]{2,1,0:T(8,128)S(1)}, f32[2,64,256]{2,1,0:T(8,128)S(1)}, u32[]{:S(2)}, u32[]{:S(2)}) collective-permute-start(f32[2,64,256]{2,1,0:T(8,128)S(1)} %aggregate.1.own), channel_id=1, source_target_pairs={{0,1},{1,0},{2,3},{3,2},{4,5},{5,4},{6,7},{7,6},{8,9},{9,8},{10,11... | collective-permute-start | bytes 393224 | tf_op jit(solution)/shard_map/ppermute | solution.py:209
  7.1 1.0 %collective-permute-done.other = f32[2,64,256]{2,1,0:T(8,128)S(1)} collective-permute-done((f32[2,64,256]{2,1,0:T(8,128)S(1)}, f32[2,64,256]{2,1,0:T(8,128)S(1)}, u32[]{:S(2)}, u32[]{:S(2)}) %collective-permute-start) | collective-permute-done | bytes 131104 | tf_op jit(solution)/shard_map/ppermute | solution.py:209
  8.1 3.0 %collective-permute-start.1 = (f32[4,16,256]{2,1,0:T(8,128)S(1)}, f32[4,16,256]{2,1,0:T(8,128)S(1)}, u32[]{:S(2)}, u32[]{:S(2)}) collective-permute-start(f32[4,16,256]{2,1,0:T(8,128)S(1)} %get-tuple-element.10), channel_id=1, source_target_pairs={{0,8},{1,3},{2,10},{3,1},{4,12},{5,7},{6,14},{7,5},{8,0},{9,11},{1... | collective-permute-start | bytes 196616 | tf_op jit(solution)/shard_map/ppermute | solution.py:209
  11.1 2.6 %collective-permute-start.2 = (f32[4,16,256]{2,1,0:T(8,128)S(1)}, f32[4,16,256]{2,1,0:T(8,128)S(1)}, u32[]{:S(2)}, u32[]{:S(2)}) collective-permute-start(f32[4,16,256]{2,1,0:T(8,128)S(1)} %get-tuple-element.11), channel_id=1, source_target_pairs={{0,16},{1,5},{2,18},{3,7},{4,20},{5,1},{6,22},{7,3},{8,24},{9,13},... | collective-permute-start | bytes 196616 | tf_op jit(solution)/shard_map/ppermute | solution.py:209
  13.6 0.0 collective-permute-start.3
  13.7 0.0 collective-permute-done.1
  13.7 3.2 %collective-permute-done.2 = f32[4,16,256]{2,1,0:T(8,128)S(1)} collective-permute-done((f32[4,16,256]{2,1,0:T(8,128)S(1)}, f32[4,16,256]{2,1,0:T(8,128)S(1)}, u32[]{:S(2)}, u32[]{:S(2)}) %collective-permute-start.2) | collective-permute-done | bytes 65568 | tf_op jit(solution)/shard_map/ppermute | solution.py:209
  16.9 2.8 %collective-permute-done.3 = f32[4,16,256]{2,1,0:T(8,128)S(1)} collective-permute-done((f32[4,16,256]{2,1,0:T(8,128)S(1)}, f32[4,16,256]{2,1,0:T(8,128)S(1)}, u32[]{:S(2)}, u32[]{:S(2)}) %collective-permute-start.3) | collective-permute-done | bytes 65568 | tf_op jit(solution)/shard_map/ppermute | solution.py:209
  19.7 3.3 %collective-permute-start.6 = (f32[16,16,256]{2,1,0:T(8,128)S(1)}, f32[16,16,256]{2,1,0:T(8,128)S(1)}, u32[]{:S(2)}, u32[]{:S(2)}) collective-permute-start(f32[16,16,256]{2,1,0:T(8,128)S(1)} %constant_dynamic-update-slice_fusion.refs_0_), channel_id=1, source_target_pairs={{0,6},{1,25},{2,4},{3,27},{4,2},{5,29},{6,0},{7,31},{8,14},{9,17},... | collective-permute-start | bytes 786440 | tf_op jit(solution)/shard_map/ppermute | solution.py:209
  23.0 0.0 collective-permute-start.5
  23.0 0.6 %collective-permute-start.4 = (f32[16,16,256]{2,1,0:T(8,128)S(1)}, f32[16,16,256]{2,1,0:T(8,128)S(1)}, u32[]{:S(2)}, u32[]{:S(2)}) collective-permute-start(f32[16,16,256]{2,1,0:T(8,128)S(1)} %constant_dynamic-update-slice_fusion.refs_0_), channel_id=1, source_target_pairs={{0,2},{1,9},{2,0},{3,11},{4,6},{5,13},{6,4},{7,15},{8,10},{9,1},{1... | collective-permute-start | bytes 786440 | tf_op jit(solution)/shard_map/ppermute | solution.py:209
  23.7 3.8 %collective-permute-done.6.refs_3_ = f32[16,16,256]{2,1,0:T(8,128)S(1)} collective-permute-done((f32[16,16,256]{2,1,0:T(8,128)S(1)}, f32[16,16,256]{2,1,0:T(8,128)S(1)}, u32[]{:S(2)}, u32[]{:S(2)}) %collective-permute-start.6) | collective-permute-done | bytes 262176 | tf_op jit(solution)/shard_map/ppermute | solution.py:209
  27.5 2.7 %collective-permute-done.5.refs_2_ = f32[16,16,256]{2,1,0:T(8,128)S(1)} collective-permute-done((f32[16,16,256]{2,1,0:T(8,128)S(1)}, f32[16,16,256]{2,1,0:T(8,128)S(1)}, u32[]{:S(2)}, u32[]{:S(2)}) %collective-permute-start.5) | collective-permute-done | bytes 262176 | tf_op jit(solution)/shard_map/ppermute | solution.py:209
  30.2 0.7 %collective-permute-start.9 = (f32[16,16,256]{2,1,0:T(8,128)S(1)}, f32[16,16,256]{2,1,0:T(8,128)S(1)}, u32[]{:S(2)}, u32[]{:S(2)}) collective-permute-start(f32[16,16,256]{2,1,0:T(8,128)S(1)} %collective-permute-done.5.refs_2_), channel_id=1, source_target_pairs={{0,1},{1,0},{2,3},{3,2},{4,5},{5,4},{6,7},{7,6},{8,9},{9,8},{10,11... | collective-permute-start | bytes 786440 | tf_op jit(solution)/shard_map/ppermute | solution.py:209
  30.8 0.0 collective-permute-start.8
  30.8 10.7 %load.1.refs_8_ = f32[4096,2048]{1,0:T(8,128)S(1)} custom-call(f32[4096,2048]{1,0:T(8,128)} %source.1), custom_call_target="tpu_custom_call" | custom-call | bytes 33554432 | tf_op jit(solution)/shard_map/load/pallas_call | solution.py:95
  41.6 0.0 collective-permute-done.10.refs_7_
  41.6 12.2 %update.1 = f32[4096,2048]{1,0:T(8,128)} custom-call(f32[16,16,256]{2,1,0:T(8,128)S(1)} %constant_dynamic-update-slice_fusion.refs_0_, f32[16,16,256]{2,1,0:T(8,128)S(1)} %collective-permute-done.4.refs_1_, f32[16,16,256]{2,1,0:T(8,128)S(1)} %collective-permute-done.5.refs_2_, f32[16,16,256]{2,1,0:T(8,128)S(1)} %collective-permute-done.6.refs_3_, ...), custom_call_target="tpu_custom_call" | custom-call | tf_op jit(solution)/shard_map/update/pallas_call | solution.py:178
  (16 shorter events, 0.1 us)
Async XLA Ops:
  0.0 1.7 %copy-start = (bf16[2,2400,256]{2,1,0:T(8,128)(2,1)S(1)}, bf16[2,2400,256]{2,1,0:T(8,128)(2,1)}, u32[]{:S(2)}) copy-start(bf16[2,2400,256]{2,1,0:T(8,128)(2,1)} %features.1) | copy-start | bytes 7372804
  1.7 0.9 %copy-start.1 = (s32[2,4,2400]{2,1,0:T(4,128)S(1)}, s32[2,4,2400]{2,1,0:T(4,128)}, u32[]{:S(2)}) copy-start(s32[2,4,2400]{2,1,0:T(4,128)} %ids.1) | copy-start | bytes 230404
  2.6 0.8 %copy-start.2 = (bf16[2,4,2400]{2,1,0:T(4,128)(2,1)S(1)}, bf16[2,4,2400]{2,1,0:T(4,128)(2,1)}, u32[]{:S(2)}) copy-start(bf16[2,4,2400]{2,1,0:T(4,128)(2,1)} %weights.1) | copy-start | bytes 115204
  3.4 0.8 %copy-start.3 = (bf16[64,256]{1,0:T(8,128)(2,1)S(1)}, bf16[64,256]{1,0:T(8,128)(2,1)}, u32[]{:S(2)}) copy-start(bf16[64,256]{1,0:T(8,128)(2,1)} %centroids.1) | copy-start | bytes 98308
  4.1 0.7 %copy-start.4 = (s32[2]{0:T(128)S(1)}, s32[2]{0:T(128)}, u32[]{:S(2)}) copy-start(s32[2]{0:T(128)} %counts.1) | copy-start | bytes 28
  6.5 1.5 %collective-permute-start = (f32[2,64,256]{2,1,0:T(8,128)S(1)}, f32[2,64,256]{2,1,0:T(8,128)S(1)}, u32[]{:S(2)}, u32[]{:S(2)}) collective-permute-start(f32[2,64,256]{2,1,0:T(8,128)S(1)} %aggregate.1.own), channel_id=1, source_target_pairs={{0,1},{1,0},{2,3},{3,2},{4,5},{5,4},{6,7},{7,6},{8,9},{9,8},{10,11... | collective-permute-start | bytes 393224 | tf_op jit(solution)/shard_map/ppermute | solution.py:209
  8.1 5.6 %collective-permute-start.1 = (f32[4,16,256]{2,1,0:T(8,128)S(1)}, f32[4,16,256]{2,1,0:T(8,128)S(1)}, u32[]{:S(2)}, u32[]{:S(2)}) collective-permute-start(f32[4,16,256]{2,1,0:T(8,128)S(1)} %get-tuple-element.10), channel_id=1, source_target_pairs={{0,8},{1,3},{2,10},{3,1},{4,12},{5,7},{6,14},{7,5},{8,0},{9,11},{1... | collective-permute-start | bytes 196616 | tf_op jit(solution)/shard_map/ppermute | solution.py:209
  11.1 5.9 %collective-permute-start.2 = (f32[4,16,256]{2,1,0:T(8,128)S(1)}, f32[4,16,256]{2,1,0:T(8,128)S(1)}, u32[]{:S(2)}, u32[]{:S(2)}) collective-permute-start(f32[4,16,256]{2,1,0:T(8,128)S(1)} %get-tuple-element.11), channel_id=1, source_target_pairs={{0,16},{1,5},{2,18},{3,7},{4,20},{5,1},{6,22},{7,3},{8,24},{9,13},... | collective-permute-start | bytes 196616 | tf_op jit(solution)/shard_map/ppermute | solution.py:209
  13.6 6.1 %collective-permute-start.3 = (f32[4,16,256]{2,1,0:T(8,128)S(1)}, f32[4,16,256]{2,1,0:T(8,128)S(1)}, u32[]{:S(2)}, u32[]{:S(2)}) collective-permute-start(f32[4,16,256]{2,1,0:T(8,128)S(1)} %get-tuple-element.12), channel_id=1, source_target_pairs={{0,24},{1,7},{2,26},{3,5},{4,28},{5,3},{6,30},{7,1},{8,16},{9,15},... | collective-permute-start | bytes 196616 | tf_op jit(solution)/shard_map/ppermute | solution.py:209
  19.7 7.7 %collective-permute-start.6 = (f32[16,16,256]{2,1,0:T(8,128)S(1)}, f32[16,16,256]{2,1,0:T(8,128)S(1)}, u32[]{:S(2)}, u32[]{:S(2)}) collective-permute-start(f32[16,16,256]{2,1,0:T(8,128)S(1)} %constant_dynamic-update-slice_fusion.refs_0_), channel_id=1, source_target_pairs={{0,6},{1,25},{2,4},{3,27},{4,2},{5,29},{6,0},{7,31},{8,14},{9,17},... | collective-permute-start | bytes 786440 | tf_op jit(solution)/shard_map/ppermute | solution.py:209
  23.0 7.2 %collective-permute-start.5 = (f32[16,16,256]{2,1,0:T(8,128)S(1)}, f32[16,16,256]{2,1,0:T(8,128)S(1)}, u32[]{:S(2)}, u32[]{:S(2)}) collective-permute-start(f32[16,16,256]{2,1,0:T(8,128)S(1)} %constant_dynamic-update-slice_fusion.refs_0_), channel_id=1, source_target_pairs={{0,4},{1,17},{2,6},{3,19},{4,0},{5,21},{6,2},{7,23},{8,12},{9,25},... | collective-permute-start | bytes 786440 | tf_op jit(solution)/shard_map/ppermute | solution.py:209
  23.0 7.8 %collective-permute-start.4 = (f32[16,16,256]{2,1,0:T(8,128)S(1)}, f32[16,16,256]{2,1,0:T(8,128)S(1)}, u32[]{:S(2)}, u32[]{:S(2)}) collective-permute-start(f32[16,16,256]{2,1,0:T(8,128)S(1)} %constant_dynamic-update-slice_fusion.refs_0_), channel_id=1, source_target_pairs={{0,2},{1,9},{2,0},{3,11},{4,6},{5,13},{6,4},{7,15},{8,10},{9,1},{1... | collective-permute-start | bytes 786440 | tf_op jit(solution)/shard_map/ppermute | solution.py:209
  23.7 17.9 %collective-permute-start.7 = (f32[16,16,256]{2,1,0:T(8,128)S(1)}, f32[16,16,256]{2,1,0:T(8,128)S(1)}, u32[]{:S(2)}, u32[]{:S(2)}) collective-permute-start(f32[16,16,256]{2,1,0:T(8,128)S(1)} %constant_dynamic-update-slice_fusion.refs_0_), channel_id=1, source_target_pairs={{0,1},{1,0},{2,3},{3,2},{4,5},{5,4},{6,7},{7,6},{8,9},{9,8},{10,11... | collective-permute-start | bytes 786440 | tf_op jit(solution)/shard_map/ppermute | solution.py:209
  27.4 14.1 %collective-permute-start.10 = (f32[16,16,256]{2,1,0:T(8,128)S(1)}, f32[16,16,256]{2,1,0:T(8,128)S(1)}, u32[]{:S(2)}, u32[]{:S(2)}) collective-permute-start(f32[16,16,256]{2,1,0:T(8,128)S(1)} %collective-permute-done.6.refs_3_), channel_id=1, source_target_pairs={{0,1},{1,0},{2,3},{3,2},{4,5},{5,4},{6,7},{7,6},{8,9},{9,8},{10,11... | collective-permute-start | bytes 786440 | tf_op jit(solution)/shard_map/ppermute | solution.py:209
  30.2 11.4 %collective-permute-start.9 = (f32[16,16,256]{2,1,0:T(8,128)S(1)}, f32[16,16,256]{2,1,0:T(8,128)S(1)}, u32[]{:S(2)}, u32[]{:S(2)}) collective-permute-start(f32[16,16,256]{2,1,0:T(8,128)S(1)} %collective-permute-done.5.refs_2_), channel_id=1, source_target_pairs={{0,1},{1,0},{2,3},{3,2},{4,5},{5,4},{6,7},{7,6},{8,9},{9,8},{10,11... | collective-permute-start | bytes 786440 | tf_op jit(solution)/shard_map/ppermute | solution.py:209
  30.8 10.7 %collective-permute-start.8 = (f32[16,16,256]{2,1,0:T(8,128)S(1)}, f32[16,16,256]{2,1,0:T(8,128)S(1)}, u32[]{:S(2)}, u32[]{:S(2)}) collective-permute-start(f32[16,16,256]{2,1,0:T(8,128)S(1)} %collective-permute-done.4.refs_1_), channel_id=1, source_target_pairs={{0,1},{1,0},{2,3},{3,2},{4,5},{5,4},{6,7},{7,6},{8,9},{9,8},{10,11... | collective-permute-start | bytes 786440 | tf_op jit(solution)/shard_map/ppermute | solution.py:209

commit v2 on v1

--- a/solution.py
+++ b/solution.py
@@ -12,43 +12,59 @@
 F32 = jnp.float32
 
 
-def aggregate_kernel(counts, ids, weights, centroids, features, rows):
-    image = pl.program_id(0)
-    top, slots = ids.shape[1:]
+def aggregate_kernel(counts, ids_in, weights_in, centroids_in, features_in, rows, *scratch):
+    ids, weights, centroids, features, sems = scratch
+    images, top, slots = ids.shape
     clusters = centroids.shape[0]
+    small = [
+        pltpu.make_async_copy(source, target, sems.at[n])
+        for n, (source, target) in enumerate(
+            [(ids_in, ids), (weights_in, weights), (centroids_in, centroids)]
+        )
+    ]
+    large = [
+        pltpu.make_async_copy(features_in.at[n], features.at[n], sems.at[len(small) + n])
+        for n in range(images)
+    ]
+    for copy in small + large:
+        copy.start()
+    for copy in small:
+        copy.wait()
+    labels = lax.broadcasted_iota(jnp.int32, (clusters, slots), 0)
     position = lax.broadcasted_iota(jnp.int32, (top, slots), 1)
-    valid_ids = jnp.where(position < counts[image], ids[0], -1)
-    values = weights[0].astype(F32)
-    labels = lax.broadcasted_iota(jnp.int32, (clusters, slots), 0)
-    assign = jnp.zeros((clusters, slots), F32)
-    for slot in range(top):
-        matched = valid_ids[slot : slot + 1] == labels
-        assign = assign + jnp.where(matched, values[slot : slot + 1], 0.0)
-    assign = assign.astype(BF16)
-    weight_sum = jnp.sum(assign.astype(F32), axis=1, keepdims=True)
-    residual = jnp.dot(assign, features[0], preferred_element_type=F32)
-    residual = residual - weight_sum * centroids[...].astype(F32)
-    square = jnp.sum(residual * residual, axis=1, keepdims=True)
-    rows[0] = residual / jnp.sqrt(square + 1e-06)
+    for image in range(images):
+        valid_ids = jnp.where(position < counts[image], ids[image], -1)
+        values = weights[image].astype(F32)
+        assign = jnp.zeros((clusters, slots), F32)
+        for slot in range(top):
+            matched = valid_ids[slot : slot + 1] == labels
+            assign = assign + jnp.where(matched, values[slot : slot + 1], 0.0)
+        assign = assign.astype(BF16)
+        weight_sum = jnp.sum(assign.astype(F32), axis=1, keepdims=True)
+        large[image].wait()
+        residual = jnp.dot(assign, features[image], preferred_element_type=F32)
+        residual = residual - weight_sum * centroids[...].astype(F32)
+        square = jnp.sum(residual * residual, axis=1, keepdims=True)
+        rows[image] = residual / jnp.sqrt(square + 1e-06)
 
 
 def aggregate(features, cluster_ids, soft_weights, counts, centroids):
-    images, slots, width = features.shape
-    top = cluster_ids.shape[1]
+    images, _, width = features.shape
     clusters = centroids.shape[0]
     return pl.pallas_call(
         aggregate_kernel,
-        grid=(images,),
-        in_specs=[
-            pl.BlockSpec(memory_space=pltpu.SMEM),
-            pl.BlockSpec((1, top, slots), lambda i: (i, 0, 0)),
-            pl.BlockSpec((1, top, slots), lambda i: (i, 0, 0)),
-            pl.BlockSpec((clusters, width), lambda i: (0, 0)),
-            pl.BlockSpec((1, slots, width), lambda i: (i, 0, 0)),
+        in_specs=[pl.BlockSpec(memory_space=pltpu.SMEM)]
+        + [pl.BlockSpec(memory_space=pltpu.HBM)] * 4,
+        out_specs=pl.BlockSpec(memory_space=VMEM),
+        out_shape=VMEM((images, clusters, width), F32),
+        scratch_shapes=[
+            VMEM(cluster_ids.shape, cluster_ids.dtype),
+            VMEM(soft_weights.shape, soft_weights.dtype),
+            VMEM(centroids.shape, centroids.dtype),
+            VMEM(features.shape, features.dtype),
+            pltpu.SemaphoreType.DMA((3 + images,)),
         ],
-        out_specs=pl.BlockSpec((1, clusters, width), lambda i: (i, 0, 0)),
-        out_shape=jax.ShapeDtypeStruct((images, clusters, width), F32),
-        compiler_params=pltpu.CompilerParams(vmem_limit_bytes=16 << 20),
+        compiler_params=pltpu.CompilerParams(vmem_limit_bytes=64000000),
         name="aggregate",
     )(counts, cluster_ids, soft_weights, centroids, features)
 
@@ -71,37 +87,9 @@
         out_specs=[pl.BlockSpec(memory_space=VMEM)] * peers,
         out_shape=[jax.ShapeDtypeStruct((2 * images, block, width), F32)] * peers,
         compiler_params=pltpu.CompilerParams(vmem_limit_bytes=4 << 20),
+        cost_estimate=pl.CostEstimate(flops=10**11, bytes_accessed=10**9, transcendentals=0),
         name="pack",
     )(own, other)
-
-
-def load_kernel(block, source, target, sems):
-    steps = source.shape[0] // block
-    copies = [
-        pltpu.make_async_copy(
-            source.at[pl.ds(i * block, block)], target.at[pl.ds(i * block, block)], sems.at[i]
-        )
-        for i in range(steps)
-    ]
-    for copy in copies:
-        copy.start()
-    for copy in copies:
-        copy.wait()
-
-
-def load(covariance, block):
-    rows, cols = covariance.shape
-    size = rows * cols * 4
-    return pl.pallas_call(
-        functools.partial(load_kernel, block),
-        in_specs=[pl.BlockSpec(memory_space=pl.ANY)],
-        out_specs=pl.BlockSpec(memory_space=VMEM),
-        out_shape=VMEM((rows, cols), F32),
-        scratch_shapes=[pltpu.SemaphoreType.DMA((rows // block,))],
-        compiler_params=pltpu.CompilerParams(vmem_limit_bytes=1 << 20),
-        cost_estimate=pl.CostEstimate(flops=0, bytes_accessed=size, transcendentals=0),
-        name="load",
-    )(covariance)
 
 
 def split(value):
@@ -226,12 +214,14 @@
     gathered = jnp.concatenate(received, axis=0)
     mine = [gathered]
     for k in range(1, peers):
-        mine.append(second(gathered, k))
+        if k % 2 and k > 1:
+            mine.append(second(mine[k - 1], 1))
+        else:
+            mine.append(second(gathered, k))
     theirs = []
     for k in range(peers):
         theirs.append(to_other(mine[k]))
-    held = load(covariance, 2 * width)
-    return update(mine, theirs, held, factor)
+    return update(mine, theirs, covariance, factor)
 
 
 def solution(mesh):

time: 54.1 us -> 43.7 us (0.81)
  Pallas kernels: 24.6 us -> 16 us
  local copies, waits for them, and re-layouts: 4.79 us -> 0.03 us
  waiting for transfers between devices: 13.5 us -> 15.2 us
  starting transfers between devices: 10.7 us -> 12.3 us
    pallas_call x2 -> x1, Pallas kernels: 12.4 us -> 3.83 us  [aggregate(): pl.pallas_call(aggregate_kernel, in_specs=[pl.BlockSpec(memory_space=pltp...]
    unnamed x13 -> x5, local copies, waits for them, and re-layouts: 4.78 us -> 0.02 us
    ppermute x11, waiting for transfers between devices: 13.5 us -> 15.2 us  [send(): return lax.ppermute(value, ('img', 'tile'), pairs)]
    ppermute x11, starting transfers between devices: 10.7 us -> 12.3 us  [send(): return lax.ppermute(value, ('img', 'tile'), pairs)]
  transfers between devices with their start and end apart: 11 -> 11, of which waited for: 5 -> 6; matrix products, arithmetic and copies ran while one was open for 0% -> 0% of each run, Pallas kernels for 20% -> 0%
where the time goes in v2:
time: 43.7 us; the launch traced here: 43.5 us
  Pallas kernels  16 us (37%)
  waiting for transfers between devices  15.2 us (35%)
  starting transfers between devices  12.3 us (28%)
    ppermute x11, waiting for transfers between devices, send(): return lax.ppermute(value, ('img', 'tile'), pairs)  15.2 us
    ppermute x11, starting transfers between devices, send(): return lax.ppermute(value, ('img', 'tile'), pairs)  12.3 us
    pallas_call x1, Pallas kernels, update(): pl.pallas_call(functools.partial(update_kernel, peers, factor, stages), i...  12.2 us
    pallas_call x1, Pallas kernels, aggregate(): pl.pallas_call(aggregate_kernel, in_specs=[pl.BlockSpec(memory_space=pltp...  3.83 us
  transfers between devices with their start and end apart: 11, of which 6 were waited for; matrix products, arithmetic and copies ran while one was open for 0% of the time, Pallas kernels for 0%

profile of v2, /device:TPU:0, one launch (start us, length us, event | category | flops | bytes accessed | tf_op | source)
XLA Modules:
  0.0 43.5 jit_solution(4920577435805534193)
XLA Ops:
  0.0 3.8 %aggregate.1.own = f32[2,64,256]{2,1,0:T(8,128)S(1)} custom-call(s32[2]{0:T(128)} %counts.1, s32[2,4,2400]{2,1,0:T(4,128)} %ids_in.1, bf16[2,4,2400]{2,1,0:T(4,128)(2,1)} %weights_in.1, bf16[64,256]{1,0:T(8,128)(2,1)} %centroids_in.1, bf16[2,2400,256]{2,1,0:T(8,128)(2,1)} %features_in.1), custom_call_target="tpu_custom_call" | custom-call | tf_op jit(solution)/shard_map/aggregate/pallas_call | solution.py:54
  3.8 0.0 copy-start
  3.9 0.6 %collective-permute-start = (f32[2,64,256]{2,1,0:T(8,128)S(1)}, f32[2,64,256]{2,1,0:T(8,128)S(1)}, u32[]{:S(2)}, u32[]{:S(2)}) collective-permute-start(f32[2,64,256]{2,1,0:T(8,128)S(1)} %aggregate.1.own), channel_id=1, source_target_pairs={{0,1},{1,0},{2,3},{3,2},{4,5},{5,4},{6,7},{7,6},{8,9},{9,8},{10,11... | collective-permute-start | bytes 393224 | tf_op jit(solution)/shard_map/ppermute | solution.py:197
  4.4 1.0 %collective-permute-done.other = f32[2,64,256]{2,1,0:T(8,128)S(1)} collective-permute-done((f32[2,64,256]{2,1,0:T(8,128)S(1)}, f32[2,64,256]{2,1,0:T(8,128)S(1)}, u32[]{:S(2)}, u32[]{:S(2)}) %collective-permute-start) | collective-permute-done | bytes 131104 | tf_op jit(solution)/shard_map/ppermute | solution.py:197
  5.4 3.0 %collective-permute-start.1 = (f32[4,16,256]{2,1,0:T(8,128)S(1)}, f32[4,16,256]{2,1,0:T(8,128)S(1)}, u32[]{:S(2)}, u32[]{:S(2)}) collective-permute-start(f32[4,16,256]{2,1,0:T(8,128)S(1)} %get-tuple-element.10), channel_id=1, source_target_pairs={{0,8},{1,3},{2,10},{3,1},{4,12},{5,7},{6,14},{7,5},{8,0},{9,11},{1... | collective-permute-start | bytes 196616 | tf_op jit(solution)/shard_map/ppermute | solution.py:197
  8.4 2.6 %collective-permute-start.2 = (f32[4,16,256]{2,1,0:T(8,128)S(1)}, f32[4,16,256]{2,1,0:T(8,128)S(1)}, u32[]{:S(2)}, u32[]{:S(2)}) collective-permute-start(f32[4,16,256]{2,1,0:T(8,128)S(1)} %get-tuple-element.11), channel_id=1, source_target_pairs={{0,16},{1,5},{2,18},{3,7},{4,20},{5,1},{6,22},{7,3},{8,24},{9,13},... | collective-permute-start | bytes 196616 | tf_op jit(solution)/shard_map/ppermute | solution.py:197
  11.0 0.0 collective-permute-start.3
  11.0 0.0 collective-permute-done.1
  11.0 3.2 %collective-permute-done.2 = f32[4,16,256]{2,1,0:T(8,128)S(1)} collective-permute-done((f32[4,16,256]{2,1,0:T(8,128)S(1)}, f32[4,16,256]{2,1,0:T(8,128)S(1)}, u32[]{:S(2)}, u32[]{:S(2)}) %collective-permute-start.2) | collective-permute-done | bytes 65568 | tf_op jit(solution)/shard_map/ppermute | solution.py:197
  14.3 2.8 %collective-permute-done.3 = f32[4,16,256]{2,1,0:T(8,128)S(1)} collective-permute-done((f32[4,16,256]{2,1,0:T(8,128)S(1)}, f32[4,16,256]{2,1,0:T(8,128)S(1)}, u32[]{:S(2)}, u32[]{:S(2)}) %collective-permute-start.3) | collective-permute-done | bytes 65568 | tf_op jit(solution)/shard_map/ppermute | solution.py:197
  17.1 1.6 %collective-permute-start.5 = (f32[16,16,256]{2,1,0:T(8,128)S(1)}, f32[16,16,256]{2,1,0:T(8,128)S(1)}, u32[]{:S(2)}, u32[]{:S(2)}) collective-permute-start(f32[16,16,256]{2,1,0:T(8,128)S(1)} %constant_dynamic-update-slice_fusion.refs_0_), channel_id=1, source_target_pairs={{0,4},{1,17},{2,6},{3,19},{4,0},{5,21},{6,2},{7,23},{8,12},{9,25},... | collective-permute-start | bytes 786440 | tf_op jit(solution)/shard_map/ppermute | solution.py:197
  18.7 2.2 %collective-permute-start.4 = (f32[16,16,256]{2,1,0:T(8,128)S(1)}, f32[16,16,256]{2,1,0:T(8,128)S(1)}, u32[]{:S(2)}, u32[]{:S(2)}) collective-permute-start(f32[16,16,256]{2,1,0:T(8,128)S(1)} %constant_dynamic-update-slice_fusion.refs_0_), channel_id=1, source_target_pairs={{0,2},{1,9},{2,0},{3,11},{4,6},{5,13},{6,4},{7,15},{8,10},{9,1},{1... | collective-permute-start | bytes 786440 | tf_op jit(solution)/shard_map/ppermute | solution.py:197
  20.9 2.6 %collective-permute-done.5.refs_2_ = f32[16,16,256]{2,1,0:T(8,128)S(1)} collective-permute-done((f32[16,16,256]{2,1,0:T(8,128)S(1)}, f32[16,16,256]{2,1,0:T(8,128)S(1)}, u32[]{:S(2)}, u32[]{:S(2)}) %collective-permute-start.5) | collective-permute-done | bytes 262176 | tf_op jit(solution)/shard_map/ppermute | solution.py:197
  23.4 1.8 %collective-permute-start.6 = (f32[16,16,256]{2,1,0:T(8,128)S(1)}, f32[16,16,256]{2,1,0:T(8,128)S(1)}, u32[]{:S(2)}, u32[]{:S(2)}) collective-permute-start(f32[16,16,256]{2,1,0:T(8,128)S(1)} %collective-permute-done.5.refs_2_), channel_id=1, source_target_pairs={{0,2},{1,9},{2,0},{3,11},{4,6},{5,13},{6,4},{7,15},{8,10},{9,1},{1... | collective-permute-start | bytes 786440 | tf_op jit(solution)/shard_map/ppermute | solution.py:197
  25.2 0.0 collective-permute-start.7
  25.2 0.5 %collective-permute-start.9 = (f32[16,16,256]{2,1,0:T(8,128)S(1)}, f32[16,16,256]{2,1,0:T(8,128)S(1)}, u32[]{:S(2)}, u32[]{:S(2)}) collective-permute-start(f32[16,16,256]{2,1,0:T(8,128)S(1)} %collective-permute-done.5.refs_2_), channel_id=1, source_target_pairs={{0,1},{1,0},{2,3},{3,2},{4,5},{5,4},{6,7},{7,6},{8,9},{9,8},{10,11... | collective-permute-start | bytes 786440 | tf_op jit(solution)/shard_map/ppermute | solution.py:197
  25.7 0.0 collective-permute-done.4.refs_1_
  25.7 0.0 collective-permute-start.8
  25.7 4.1 %collective-permute-done.6.refs_3_ = f32[16,16,256]{2,1,0:T(8,128)S(1)} collective-permute-done((f32[16,16,256]{2,1,0:T(8,128)S(1)}, f32[16,16,256]{2,1,0:T(8,128)S(1)}, u32[]{:S(2)}, u32[]{:S(2)}) %collective-permute-start.6) | collective-permute-done | bytes 262176 | tf_op jit(solution)/shard_map/ppermute | solution.py:197
  29.8 0.0 collective-permute-start.10
  29.8 0.0 collective-permute-done.7.refs_4_
  29.8 0.0 collective-permute-done.9.refs_6_
  29.8 1.5 %collective-permute-done.10.refs_7_ = f32[16,16,256]{2,1,0:T(8,128)S(1)} collective-permute-done((f32[16,16,256]{2,1,0:T(8,128)S(1)}, f32[16,16,256]{2,1,0:T(8,128)S(1)}, u32[]{:S(2)}, u32[]{:S(2)}) %collective-permute-start.10) | collective-permute-done | bytes 262176 | tf_op jit(solution)/shard_map/ppermute | solution.py:197
  31.4 12.2 %update.1 = f32[4096,2048]{1,0:T(8,128)} custom-call(f32[16,16,256]{2,1,0:T(8,128)S(1)} %constant_dynamic-update-slice_fusion.refs_0_, f32[16,16,256]{2,1,0:T(8,128)S(1)} %collective-permute-done.4.refs_1_, f32[16,16,256]{2,1,0:T(8,128)S(1)} %collective-permute-done.5.refs_2_, f32[16,16,256]{2,1,0:T(8,128)S(1)} %collective-permute-done.6.refs_3_, ...), custom_call_target="tpu_custom_call" | custom-call | tf_op jit(solution)/shard_map/update/pallas_call | solution.py:166
  (7 shorter events, 0.0 us)
Async XLA Ops:
  3.8 27.5 %copy-start = (f32[4096,2048]{1,0:T(8,128)S(1)}, f32[4096,2048]{1,0:T(8,128)}, u32[]{:S(2)}) copy-start(f32[4096,2048]{1,0:T(8,128)} %refs_8_.1) | copy-start | bytes 100663296
  3.9 1.5 %collective-permute-start = (f32[2,64,256]{2,1,0:T(8,128)S(1)}, f32[2,64,256]{2,1,0:T(8,128)S(1)}, u32[]{:S(2)}, u32[]{:S(2)}) collective-permute-start(f32[2,64,256]{2,1,0:T(8,128)S(1)} %aggregate.1.own), channel_id=1, source_target_pairs={{0,1},{1,0},{2,3},{3,2},{4,5},{5,4},{6,7},{7,6},{8,9},{9,8},{10,11... | collective-permute-start | bytes 393224 | tf_op jit(solution)/shard_map/ppermute | solution.py:197
  5.4 5.6 %collective-permute-start.1 = (f32[4,16,256]{2,1,0:T(8,128)S(1)}, f32[4,16,256]{2,1,0:T(8,128)S(1)}, u32[]{:S(2)}, u32[]{:S(2)}) collective-permute-start(f32[4,16,256]{2,1,0:T(8,128)S(1)} %get-tuple-element.10), channel_id=1, source_target_pairs={{0,8},{1,3},{2,10},{3,1},{4,12},{5,7},{6,14},{7,5},{8,0},{9,11},{1... | collective-permute-start | bytes 196616 | tf_op jit(solution)/shard_map/ppermute | solution.py:197
  8.4 5.9 %collective-permute-start.2 = (f32[4,16,256]{2,1,0:T(8,128)S(1)}, f32[4,16,256]{2,1,0:T(8,128)S(1)}, u32[]{:S(2)}, u32[]{:S(2)}) collective-permute-start(f32[4,16,256]{2,1,0:T(8,128)S(1)} %get-tuple-element.11), channel_id=1, source_target_pairs={{0,16},{1,5},{2,18},{3,7},{4,20},{5,1},{6,22},{7,3},{8,24},{9,13},... | collective-permute-start | bytes 196616 | tf_op jit(solution)/shard_map/ppermute | solution.py:197
  11.0 6.1 %collective-permute-start.3 = (f32[4,16,256]{2,1,0:T(8,128)S(1)}, f32[4,16,256]{2,1,0:T(8,128)S(1)}, u32[]{:S(2)}, u32[]{:S(2)}) collective-permute-start(f32[4,16,256]{2,1,0:T(8,128)S(1)} %get-tuple-element.12), channel_id=1, source_target_pairs={{0,24},{1,7},{2,26},{3,5},{4,28},{5,3},{6,30},{7,1},{8,16},{9,15},... | collective-permute-start | bytes 196616 | tf_op jit(solution)/shard_map/ppermute | solution.py:197
  17.1 6.4 %collective-permute-start.5 = (f32[16,16,256]{2,1,0:T(8,128)S(1)}, f32[16,16,256]{2,1,0:T(8,128)S(1)}, u32[]{:S(2)}, u32[]{:S(2)}) collective-permute-start(f32[16,16,256]{2,1,0:T(8,128)S(1)} %constant_dynamic-update-slice_fusion.refs_0_), channel_id=1, source_target_pairs={{0,4},{1,17},{2,6},{3,19},{4,0},{5,21},{6,2},{7,23},{8,12},{9,25},... | collective-permute-start | bytes 786440 | tf_op jit(solution)/shard_map/ppermute | solution.py:197
  18.7 7.1 %collective-permute-start.4 = (f32[16,16,256]{2,1,0:T(8,128)S(1)}, f32[16,16,256]{2,1,0:T(8,128)S(1)}, u32[]{:S(2)}, u32[]{:S(2)}) collective-permute-start(f32[16,16,256]{2,1,0:T(8,128)S(1)} %constant_dynamic-update-slice_fusion.refs_0_), channel_id=1, source_target_pairs={{0,2},{1,9},{2,0},{3,11},{4,6},{5,13},{6,4},{7,15},{8,10},{9,1},{1... | collective-permute-start | bytes 786440 | tf_op jit(solution)/shard_map/ppermute | solution.py:197
  23.4 6.4 %collective-permute-start.6 = (f32[16,16,256]{2,1,0:T(8,128)S(1)}, f32[16,16,256]{2,1,0:T(8,128)S(1)}, u32[]{:S(2)}, u32[]{:S(2)}) collective-permute-start(f32[16,16,256]{2,1,0:T(8,128)S(1)} %collective-permute-done.5.refs_2_), channel_id=1, source_target_pairs={{0,2},{1,9},{2,0},{3,11},{4,6},{5,13},{6,4},{7,15},{8,10},{9,1},{1... | collective-permute-start | bytes 786440 | tf_op jit(solution)/shard_map/ppermute | solution.py:197
  25.2 4.6 %collective-permute-start.7 = (f32[16,16,256]{2,1,0:T(8,128)S(1)}, f32[16,16,256]{2,1,0:T(8,128)S(1)}, u32[]{:S(2)}, u32[]{:S(2)}) collective-permute-start(f32[16,16,256]{2,1,0:T(8,128)S(1)} %constant_dynamic-update-slice_fusion.refs_0_), channel_id=1, source_target_pairs={{0,1},{1,0},{2,3},{3,2},{4,5},{5,4},{6,7},{7,6},{8,9},{9,8},{10,11... | collective-permute-start | bytes 786440 | tf_op jit(solution)/shard_map/ppermute | solution.py:197
  25.2 4.6 %collective-permute-start.9 = (f32[16,16,256]{2,1,0:T(8,128)S(1)}, f32[16,16,256]{2,1,0:T(8,128)S(1)}, u32[]{:S(2)}, u32[]{:S(2)}) collective-permute-start(f32[16,16,256]{2,1,0:T(8,128)S(1)} %collective-permute-done.5.refs_2_), channel_id=1, source_target_pairs={{0,1},{1,0},{2,3},{3,2},{4,5},{5,4},{6,7},{7,6},{8,9},{9,8},{10,11... | collective-permute-start | bytes 786440 | tf_op jit(solution)/shard_map/ppermute | solution.py:197
  25.7 4.1 %collective-permute-start.8 = (f32[16,16,256]{2,1,0:T(8,128)S(1)}, f32[16,16,256]{2,1,0:T(8,128)S(1)}, u32[]{:S(2)}, u32[]{:S(2)}) collective-permute-start(f32[16,16,256]{2,1,0:T(8,128)S(1)} %collective-permute-done.4.refs_1_), channel_id=1, source_target_pairs={{0,1},{1,0},{2,3},{3,2},{4,5},{5,4},{6,7},{7,6},{8,9},{9,8},{10,11... | collective-permute-start | bytes 786440 | tf_op jit(solution)/shard_map/ppermute | solution.py:197
  29.8 1.5 %collective-permute-start.10 = (f32[16,16,256]{2,1,0:T(8,128)S(1)}, f32[16,16,256]{2,1,0:T(8,128)S(1)}, u32[]{:S(2)}, u32[]{:S(2)}) collective-permute-start(f32[16,16,256]{2,1,0:T(8,128)S(1)} %collective-permute-done.6.refs_3_), channel_id=1, source_target_pairs={{0,1},{1,0},{2,3},{3,2},{4,5},{5,4},{6,7},{7,6},{8,9},{9,8},{10,11... | collective-permute-start | bytes 786440 | tf_op jit(solution)/shard_map/ppermute | solution.py:197

commit v3 on v2

--- a/solution.py
+++ b/solution.py
@@ -12,14 +12,19 @@
 F32 = jnp.float32
 
 
-def aggregate_kernel(counts, ids_in, weights_in, centroids_in, features_in, rows, *scratch):
-    ids, weights, centroids, features, sems = scratch
+def aggregate_kernel(counts_in, ids_in, weights_in, centroids_in, features_in, rows, *scratch):
+    counts, ids, weights, centroids, features, sems = scratch
     images, top, slots = ids.shape
     clusters = centroids.shape[0]
     small = [
         pltpu.make_async_copy(source, target, sems.at[n])
         for n, (source, target) in enumerate(
-            [(ids_in, ids), (weights_in, weights), (centroids_in, centroids)]
+            [
+                (counts_in, counts),
+                (ids_in, ids),
+                (weights_in, weights),
+                (centroids_in, centroids),
+            ]
         )
     ]
     large = [
@@ -53,16 +58,16 @@
     clusters = centroids.shape[0]
     return pl.pallas_call(
         aggregate_kernel,
-        in_specs=[pl.BlockSpec(memory_space=pltpu.SMEM)]
-        + [pl.BlockSpec(memory_space=pltpu.HBM)] * 4,
+        in_specs=[pl.BlockSpec(memory_space=pltpu.HBM)] * 5,
         out_specs=pl.BlockSpec(memory_space=VMEM),
         out_shape=VMEM((images, clusters, width), F32),
         scratch_shapes=[
+            pltpu.SMEM(counts.shape, counts.dtype),
             VMEM(cluster_ids.shape, cluster_ids.dtype),
             VMEM(soft_weights.shape, soft_weights.dtype),
             VMEM(centroids.shape, centroids.dtype),
             VMEM(features.shape, features.dtype),
-            pltpu.SemaphoreType.DMA((3 + images,)),
+            pltpu.SemaphoreType.DMA((4 + images,)),
         ],
         compiler_params=pltpu.CompilerParams(vmem_limit_bytes=64000000),
         name="aggregate",
@@ -98,28 +103,33 @@
     return high, low
 
 
-def update_kernel(peers, factor, stages, *refs):
-    mine, theirs = refs[:peers], refs[peers : 2 * peers]
-    covariance, updated, left, right, stage, sems = refs[2 * peers :]
+def update_kernel(peers, factor, stages, sizes, *refs):
+    tree = [refs[sum(sizes[:n]) : sum(sizes[: n + 1])] for n in range(2 * peers)]
+    mine, theirs = tree[:peers], tree[peers:]
+    covariance, updated, left, right, stage, sems = refs[sum(sizes) :]
     core = lax.rem(lax.axis_index("tile"), 2)
-    group, block, width = mine[0].shape
+    group = sum(ref.shape[0] for ref in mine[0])
+    block, width = mine[0][0].shape[1:]
     part = group // peers
     count = group * peers
     half = block // 2
 
+    def take(pieces, slot, cluster):
+        size = pieces[0].shape[0]
+        start = slot * part
+        return pieces[start // size][start % size : start % size + part, cluster, :]
+
     def prepare(row_refs, col_refs, base):
+        slots = [(j, t) for j in range(peers) for t in range(peers)]
         for k in range(half):
-            pieces = []
-            for j in range(peers):
-                for t in range(peers):
-                    pieces.append(col_refs[t][j * part : (j + 1) * part, base + k, :])
+            pieces = [take(col_refs[t], j, base + k) for j, t in slots]
             high, low = split(jnp.concatenate(pieces, axis=0) * factor)
             columns = slice(k * width, (k + 1) * width)
             right[0 * count : 1 * count, columns] = high
             right[1 * count : 2 * count, columns] = low
             right[2 * count : 3 * count, columns] = high
         for k in range(block):
-            pieces = [row_refs[j][:, k, :] for j in range(peers)]
+            pieces = [ref[:, k, :] for refs_of in row_refs for ref in refs_of]
             high, low = split(jnp.concatenate(pieces, axis=0))
             left[k, 0 * count : 1 * count] = high
             left[k, 1 * count : 2 * count] = high
@@ -159,13 +169,15 @@
 
 def update(mine, theirs, covariance, factor):
     peers = len(mine)
-    group, block, width = mine[0].shape
-    count = group * peers
+    sizes = [len(pieces) for pieces in mine + theirs]
+    flat = [piece for pieces in mine + theirs for piece in pieces]
+    block, width = flat[0].shape[1:]
+    count = sum(piece.shape[0] for pieces in mine for piece in pieces)
     rows, cols = covariance.shape
     stages = 3
     return pl.pallas_call(
-        functools.partial(update_kernel, peers, factor, stages),
-        in_specs=[pl.BlockSpec(memory_space=VMEM)] * (2 * peers + 1),
+        functools.partial(update_kernel, peers, factor, stages, sizes),
+        in_specs=[pl.BlockSpec(memory_space=VMEM)] * (len(flat) + 1),
         out_specs=pl.BlockSpec(memory_space=pl.ANY),
         out_shape=jax.ShapeDtypeStruct((rows, cols), F32),
         scratch_shapes=[
@@ -176,7 +188,7 @@
         ],
         compiler_params=pltpu.CompilerParams(vmem_limit_bytes=12 << 20),
         name="update",
-    )(*mine, *theirs, covariance)
+    )(*flat, covariance)
 
 
 def body(features, cluster_ids, soft_weights, counts, centroids, covariance):
@@ -211,16 +223,19 @@
     received = [parts[0]]
     for k in range(1, peers):
         received.append(first(parts[k], k))
-    gathered = jnp.concatenate(received, axis=0)
+    middle = peers // 2
+    gathered = [jnp.concatenate(received[:middle]), jnp.concatenate(received[middle:])]
     mine = [gathered]
     for k in range(1, peers):
-        if k % 2 and k > 1:
-            mine.append(second(mine[k - 1], 1))
-        else:
-            mine.append(second(gathered, k))
+        low = k & -k
+        arrived = []
+        for piece in mine[k - low]:
+            arrived.append(second(piece, low))
+        mine.append(arrived)
     theirs = []
     for k in range(peers):
-        theirs.append(to_other(mine[k]))
+        pieces = mine[k] if k == peers - 1 else [jnp.concatenate(mine[k])]
+        theirs.append([to_other(piece) for piece in pieces])
     return update(mine, theirs, covariance, factor)
 
 

time: 43.7 us -> 43.5 us (level)
  starting transfers between devices: 12.3 us -> 16.8 us
  waiting for transfers between devices: 15.2 us -> 11 us
  Pallas kernels: 16 us -> 15.4 us
    ppermute x11 -> x15, starting transfers between devices: 12.3 us -> 16.8 us  [send(): return lax.ppermute(value, ('img', 'tile'), pairs)]
    ppermute x11 -> x15, waiting for transfers between devices: 15.2 us -> 11 us  [send(): return lax.ppermute(value, ('img', 'tile'), pairs)]
    pallas_call x1, Pallas kernels: 3.83 us -> 3.18 us  [aggregate(): pl.pallas_call(aggregate_kernel, in_specs=[pl.BlockSpec(memory_space=pltp...]
  transfers between devices with their start and end apart: 11 -> 15, of which waited for: 6 -> 8; matrix products, arithmetic and copies ran while one was open for 0% -> 0% of each run, Pallas kernels for 0% -> 0%
where the time goes in v3:
time: 43.5 us; the launch traced here: 43.3 us
  starting transfers between devices  16.8 us (39%)
  Pallas kernels  15.4 us (35%)
  waiting for transfers between devices  11 us (25%)
    ppermute x15, starting transfers between devices, send(): return lax.ppermute(value, ('img', 'tile'), pairs)  16.8 us
    pallas_call x1, Pallas kernels, update(): pl.pallas_call(functools.partial(update_kernel, peers, factor, stages, si...  12.2 us
    ppermute x15, waiting for transfers between devices, send(): return lax.ppermute(value, ('img', 'tile'), pairs)  11 us
    pallas_call x1, Pallas kernels, aggregate(): pl.pallas_call(aggregate_kernel, in_specs=[pl.BlockSpec(memory_space=pltp...  3.18 us
  transfers between devices with their start and end apart: 15, of which 8 were waited for; matrix products, arithmetic and copies ran while one was open for 0% of the time, Pallas kernels for 0%

profile of v3, /device:TPU:0, one launch (start us, length us, event | category | flops | bytes accessed | tf_op | source)
XLA Modules:
  0.0 43.3 jit_solution(7300745553477990370)
XLA Ops:
  0.0 3.2 %aggregate.1.own = f32[2,64,256]{2,1,0:T(8,128)S(1)} custom-call(s32[2]{0:T(128)} %counts_in.1, s32[2,4,2400]{2,1,0:T(4,128)} %ids_in.1, bf16[2,4,2400]{2,1,0:T(4,128)(2,1)} %weights_in.1, bf16[64,256]{1,0:T(8,128)(2,1)} %centroids_in.1, bf16[2,2400,256]{2,1,0:T(8,128)(2,1)} %features_in.1), custom_call_target="tpu_custom_call" | custom-call | tf_op jit(solution)/shard_map/aggregate/pallas_call | solution.py:59
  3.2 0.6 %collective-permute-start = (f32[2,64,256]{2,1,0:T(8,128)S(1)}, f32[2,64,256]{2,1,0:T(8,128)S(1)}, u32[]{:S(2)}, u32[]{:S(2)}) collective-permute-start(f32[2,64,256]{2,1,0:T(8,128)S(1)} %aggregate.1.own), channel_id=1, source_target_pairs={{0,1},{1,0},{2,3},{3,2},{4,5},{5,4},{6,7},{7,6},{8,9},{9,8},{10,11... | collective-permute-start | bytes 393224 | tf_op jit(solution)/shard_map/ppermute | solution.py:209
  3.8 1.0 %collective-permute-done.other = f32[2,64,256]{2,1,0:T(8,128)S(1)} collective-permute-done((f32[2,64,256]{2,1,0:T(8,128)S(1)}, f32[2,64,256]{2,1,0:T(8,128)S(1)}, u32[]{:S(2)}, u32[]{:S(2)}) %collective-permute-start) | collective-permute-done | bytes 131104 | tf_op jit(solution)/shard_map/ppermute | solution.py:209
  4.8 3.0 %collective-permute-start.1 = (f32[4,16,256]{2,1,0:T(8,128)S(1)}, f32[4,16,256]{2,1,0:T(8,128)S(1)}, u32[]{:S(2)}, u32[]{:S(2)}) collective-permute-start(f32[4,16,256]{2,1,0:T(8,128)S(1)} %get-tuple-element.10), channel_id=1, source_target_pairs={{0,8},{1,3},{2,10},{3,1},{4,12},{5,7},{6,14},{7,5},{8,0},{9,11},{1... | collective-permute-start | bytes 196616 | tf_op jit(solution)/shard_map/ppermute | solution.py:209
  7.8 2.6 %collective-permute-start.2 = (f32[4,16,256]{2,1,0:T(8,128)S(1)}, f32[4,16,256]{2,1,0:T(8,128)S(1)}, u32[]{:S(2)}, u32[]{:S(2)}) collective-permute-start(f32[4,16,256]{2,1,0:T(8,128)S(1)} %get-tuple-element.11), channel_id=1, source_target_pairs={{0,16},{1,5},{2,18},{3,7},{4,20},{5,1},{6,22},{7,3},{8,24},{9,13},... | collective-permute-start | bytes 196616 | tf_op jit(solution)/shard_map/ppermute | solution.py:209
  10.4 1.8 %collective-permute-start.6 = (f32[8,16,256]{2,1,0:T(8,128)S(1)}, f32[8,16,256]{2,1,0:T(8,128)S(1)}, u32[]{:S(2)}, u32[]{:S(2)}) collective-permute-start(f32[8,16,256]{2,1,0:T(8,128)S(1)} %constant_dynamic-update-slice_fusion.refs_0_), channel_id=1, source_target_pairs={{0,4},{1,17},{2,6},{3,19},{4,0},{5,21},{6,2},{7,23},{8,12},{9,25},... | collective-permute-start | bytes 393224 | tf_op jit(solution)/shard_map/ppermute | solution.py:209
  12.2 1.8 %collective-permute-done.2 = f32[4,16,256]{2,1,0:T(8,128)S(1)} collective-permute-done((f32[4,16,256]{2,1,0:T(8,128)S(1)}, f32[4,16,256]{2,1,0:T(8,128)S(1)}, u32[]{:S(2)}, u32[]{:S(2)}) %collective-permute-start.2) | collective-permute-done | bytes 65568 | tf_op jit(solution)/shard_map/ppermute | solution.py:209
  14.0 2.4 %collective-permute-done.3 = f32[4,16,256]{2,1,0:T(8,128)S(1)} collective-permute-done((f32[4,16,256]{2,1,0:T(8,128)S(1)}, f32[4,16,256]{2,1,0:T(8,128)S(1)}, u32[]{:S(2)}, u32[]{:S(2)}) %collective-permute-start.3) | collective-permute-done | bytes 65568 | tf_op jit(solution)/shard_map/ppermute | solution.py:209
  16.4 1.5 %collective-permute-start.7 = (f32[8,16,256]{2,1,0:T(8,128)S(1)}, f32[8,16,256]{2,1,0:T(8,128)S(1)}, u32[]{:S(2)}, u32[]{:S(2)}) collective-permute-start(f32[8,16,256]{2,1,0:T(8,128)S(1)} %constant_dynamic-update-slice_fusion.2.refs_1_), channel_id=1, source_target_pairs={{0,4},{1,17},{2,6},{3,19},{4,0},{5,21},{6,2},{7,23},{8,12},{9,25},... | collective-permute-start | bytes 393224 | tf_op jit(solution)/shard_map/ppermute | solution.py:209
  17.9 1.6 %collective-permute-start.4 = (f32[8,16,256]{2,1,0:T(8,128)S(1)}, f32[8,16,256]{2,1,0:T(8,128)S(1)}, u32[]{:S(2)}, u32[]{:S(2)}) collective-permute-start(f32[8,16,256]{2,1,0:T(8,128)S(1)} %constant_dynamic-update-slice_fusion.refs_0_), channel_id=1, source_target_pairs={{0,2},{1,9},{2,0},{3,11},{4,6},{5,13},{6,4},{7,15},{8,10},{9,1},{1... | collective-permute-start | bytes 393224 | tf_op jit(solution)/shard_map/ppermute | solution.py:209
  19.5 0.5 %collective-permute-start.5 = (f32[8,16,256]{2,1,0:T(8,128)S(1)}, f32[8,16,256]{2,1,0:T(8,128)S(1)}, u32[]{:S(2)}, u32[]{:S(2)}) collective-permute-start(f32[8,16,256]{2,1,0:T(8,128)S(1)} %constant_dynamic-update-slice_fusion.2.refs_1_), channel_id=1, source_target_pairs={{0,2},{1,9},{2,0},{3,11},{4,6},{5,13},{6,4},{7,15},{8,10},{9,1},{1... | collective-permute-start | bytes 393224 | tf_op jit(solution)/shard_map/ppermute | solution.py:209
  20.0 0.1 collective-permute-start.10
  20.1 1.3 %collective-permute-done.7.refs_5_ = f32[8,16,256]{2,1,0:T(8,128)S(1)} collective-permute-done((f32[8,16,256]{2,1,0:T(8,128)S(1)}, f32[8,16,256]{2,1,0:T(8,128)S(1)}, u32[]{:S(2)}, u32[]{:S(2)}) %collective-permute-start.7) | collective-permute-done | bytes 131104 | tf_op jit(solution)/shard_map/ppermute | solution.py:209
  21.4 0.1 collective-permute-start.12
  21.5 1.6 %collective-permute-start.8 = (f32[8,16,256]{2,1,0:T(8,128)S(1)}, f32[8,16,256]{2,1,0:T(8,128)S(1)}, u32[]{:S(2)}, u32[]{:S(2)}) collective-permute-start(f32[8,16,256]{2,1,0:T(8,128)S(1)} %collective-permute-done.6.refs_4_), channel_id=1, source_target_pairs={{0,2},{1,9},{2,0},{3,11},{4,6},{5,13},{6,4},{7,15},{8,10},{9,1},{1... | collective-permute-start | bytes 393224 | tf_op jit(solution)/shard_map/ppermute | solution.py:209
  23.0 1.4 %collective-permute-done.5.refs_3_ = f32[8,16,256]{2,1,0:T(8,128)S(1)} collective-permute-done((f32[8,16,256]{2,1,0:T(8,128)S(1)}, f32[8,16,256]{2,1,0:T(8,128)S(1)}, u32[]{:S(2)}, u32[]{:S(2)}) %collective-permute-start.5) | collective-permute-done | bytes 131104 | tf_op jit(solution)/shard_map/ppermute | solution.py:209
  24.5 0.1 collective-permute-start.11
  24.6 1.8 %collective-permute-start.9 = (f32[8,16,256]{2,1,0:T(8,128)S(1)}, f32[8,16,256]{2,1,0:T(8,128)S(1)}, u32[]{:S(2)}, u32[]{:S(2)}) collective-permute-start(f32[8,16,256]{2,1,0:T(8,128)S(1)} %collective-permute-done.7.refs_5_), channel_id=1, source_target_pairs={{0,2},{1,9},{2,0},{3,11},{4,6},{5,13},{6,4},{7,15},{8,10},{9,1},{1... | collective-permute-start | bytes 393224 | tf_op jit(solution)/shard_map/ppermute | solution.py:209
  26.3 0.2 collective-permute-done.8.refs_6_
  26.5 1.2 %collective-permute-start.13 = (f32[8,16,256]{2,1,0:T(8,128)S(1)}, f32[8,16,256]{2,1,0:T(8,128)S(1)}, u32[]{:S(2)}, u32[]{:S(2)}) collective-permute-start(f32[8,16,256]{2,1,0:T(8,128)S(1)} %collective-permute-done.8.refs_6_), channel_id=1, source_target_pairs={{0,1},{1,0},{2,3},{3,2},{4,5},{5,4},{6,7},{7,6},{8,9},{9,8},{10,11... | collective-permute-start | bytes 393224 | tf_op jit(solution)/shard_map/ppermute | solution.py:209
  27.8 1.8 %collective-permute-done.9.refs_7_ = f32[8,16,256]{2,1,0:T(8,128)S(1)} collective-permute-done((f32[8,16,256]{2,1,0:T(8,128)S(1)}, f32[8,16,256]{2,1,0:T(8,128)S(1)}, u32[]{:S(2)}, u32[]{:S(2)}) %collective-permute-start.9) | collective-permute-done | bytes 131104 | tf_op jit(solution)/shard_map/ppermute | solution.py:209
  29.6 0.5 %collective-permute-start.14 = (f32[8,16,256]{2,1,0:T(8,128)S(1)}, f32[8,16,256]{2,1,0:T(8,128)S(1)}, u32[]{:S(2)}, u32[]{:S(2)}) collective-permute-start(f32[8,16,256]{2,1,0:T(8,128)S(1)} %collective-permute-done.9.refs_7_), channel_id=1, source_target_pairs={{0,1},{1,0},{2,3},{3,2},{4,5},{5,4},{6,7},{7,6},{8,9},{9,8},{10,11... | collective-permute-start | bytes 393224 | tf_op jit(solution)/shard_map/ppermute | solution.py:209
  30.1 1.0 %collective-permute-done.14.refs_12_ = f32[8,16,256]{2,1,0:T(8,128)S(1)} collective-permute-done((f32[8,16,256]{2,1,0:T(8,128)S(1)}, f32[8,16,256]{2,1,0:T(8,128)S(1)}, u32[]{:S(2)}, u32[]{:S(2)}) %collective-permute-start.14) | collective-permute-done | bytes 131104 | tf_op jit(solution)/shard_map/ppermute | solution.py:209
  31.1 12.2 %update.1 = f32[4096,2048]{1,0:T(8,128)} custom-call(f32[8,16,256]{2,1,0:T(8,128)S(1)} %constant_dynamic-update-slice_fusion.refs_0_, f32[8,16,256]{2,1,0:T(8,128)S(1)} %constant_dynamic-update-slice_fusion.2.refs_1_, f32[8,16,256]{2,1,0:T(8,128)S(1)} %collective-permute-done.4.refs_2_, f32[8,16,256]{2,1,0:T(8,128)S(1)} %collective-permute-done.5.refs_3_, ...), custom_call_target="tpu_custom_call" | custom-call | tf_op jit(solution)/shard_map/update/pallas_call | solution.py:178
  (18 shorter events, 0.1 us)
Async XLA Ops:
  3.2 27.9 %copy-start = (f32[4096,2048]{1,0:T(8,128)S(1)}, f32[4096,2048]{1,0:T(8,128)}, u32[]{:S(2)}) copy-start(f32[4096,2048]{1,0:T(8,128)} %refs_13_.1) | copy-start | bytes 100663296
  3.2 1.5 %collective-permute-start = (f32[2,64,256]{2,1,0:T(8,128)S(1)}, f32[2,64,256]{2,1,0:T(8,128)S(1)}, u32[]{:S(2)}, u32[]{:S(2)}) collective-permute-start(f32[2,64,256]{2,1,0:T(8,128)S(1)} %aggregate.1.own), channel_id=1, source_target_pairs={{0,1},{1,0},{2,3},{3,2},{4,5},{5,4},{6,7},{7,6},{8,9},{9,8},{10,11... | collective-permute-start | bytes 393224 | tf_op jit(solution)/shard_map/ppermute | solution.py:209
  4.8 5.6 %collective-permute-start.1 = (f32[4,16,256]{2,1,0:T(8,128)S(1)}, f32[4,16,256]{2,1,0:T(8,128)S(1)}, u32[]{:S(2)}, u32[]{:S(2)}) collective-permute-start(f32[4,16,256]{2,1,0:T(8,128)S(1)} %get-tuple-element.10), channel_id=1, source_target_pairs={{0,8},{1,3},{2,10},{3,1},{4,12},{5,7},{6,14},{7,5},{8,0},{9,11},{1... | collective-permute-start | bytes 196616 | tf_op jit(solution)/shard_map/ppermute | solution.py:209
  7.8 6.2 %collective-permute-start.2 = (f32[4,16,256]{2,1,0:T(8,128)S(1)}, f32[4,16,256]{2,1,0:T(8,128)S(1)}, u32[]{:S(2)}, u32[]{:S(2)}) collective-permute-start(f32[4,16,256]{2,1,0:T(8,128)S(1)} %get-tuple-element.11), channel_id=1, source_target_pairs={{0,16},{1,5},{2,18},{3,7},{4,20},{5,1},{6,22},{7,3},{8,24},{9,13},... | collective-permute-start | bytes 196616 | tf_op jit(solution)/shard_map/ppermute | solution.py:209
  10.3 6.1 %collective-permute-start.3 = (f32[4,16,256]{2,1,0:T(8,128)S(1)}, f32[4,16,256]{2,1,0:T(8,128)S(1)}, u32[]{:S(2)}, u32[]{:S(2)}) collective-permute-start(f32[4,16,256]{2,1,0:T(8,128)S(1)} %get-tuple-element.12), channel_id=1, source_target_pairs={{0,24},{1,7},{2,26},{3,5},{4,28},{5,3},{6,30},{7,1},{8,16},{9,15},... | collective-permute-start | bytes 196616 | tf_op jit(solution)/shard_map/ppermute | solution.py:209
  10.4 9.7 %collective-permute-start.6 = (f32[8,16,256]{2,1,0:T(8,128)S(1)}, f32[8,16,256]{2,1,0:T(8,128)S(1)}, u32[]{:S(2)}, u32[]{:S(2)}) collective-permute-start(f32[8,16,256]{2,1,0:T(8,128)S(1)} %constant_dynamic-update-slice_fusion.refs_0_), channel_id=1, source_target_pairs={{0,4},{1,17},{2,6},{3,19},{4,0},{5,21},{6,2},{7,23},{8,12},{9,25},... | collective-permute-start | bytes 393224 | tf_op jit(solution)/shard_map/ppermute | solution.py:209
  16.4 5.0 %collective-permute-start.7 = (f32[8,16,256]{2,1,0:T(8,128)S(1)}, f32[8,16,256]{2,1,0:T(8,128)S(1)}, u32[]{:S(2)}, u32[]{:S(2)}) collective-permute-start(f32[8,16,256]{2,1,0:T(8,128)S(1)} %constant_dynamic-update-slice_fusion.2.refs_1_), channel_id=1, source_target_pairs={{0,4},{1,17},{2,6},{3,19},{4,0},{5,21},{6,2},{7,23},{8,12},{9,25},... | collective-permute-start | bytes 393224 | tf_op jit(solution)/shard_map/ppermute | solution.py:209
  17.9 5.1 %collective-permute-start.4 = (f32[8,16,256]{2,1,0:T(8,128)S(1)}, f32[8,16,256]{2,1,0:T(8,128)S(1)}, u32[]{:S(2)}, u32[]{:S(2)}) collective-permute-start(f32[8,16,256]{2,1,0:T(8,128)S(1)} %constant_dynamic-update-slice_fusion.refs_0_), channel_id=1, source_target_pairs={{0,2},{1,9},{2,0},{3,11},{4,6},{5,13},{6,4},{7,15},{8,10},{9,1},{1... | collective-permute-start | bytes 393224 | tf_op jit(solution)/shard_map/ppermute | solution.py:209
  19.5 5.0 %collective-permute-start.5 = (f32[8,16,256]{2,1,0:T(8,128)S(1)}, f32[8,16,256]{2,1,0:T(8,128)S(1)}, u32[]{:S(2)}, u32[]{:S(2)}) collective-permute-start(f32[8,16,256]{2,1,0:T(8,128)S(1)} %constant_dynamic-update-slice_fusion.2.refs_1_), channel_id=1, source_target_pairs={{0,2},{1,9},{2,0},{3,11},{4,6},{5,13},{6,4},{7,15},{8,10},{9,1},{1... | collective-permute-start | bytes 393224 | tf_op jit(solution)/shard_map/ppermute | solution.py:209
  20.0 10.1 %collective-permute-start.10 = (f32[16,16,256]{2,1,0:T(8,128)S(1)}, f32[16,16,256]{2,1,0:T(8,128)S(1)}, u32[]{:S(2)}, u32[]{:S(2)}) collective-permute-start(f32[16,16,256]{2,1,0:T(8,128)S(1)} %pad_maximum_fusion), channel_id=1, source_target_pairs={{0,1},{1,0},{2,3},{3,2},{4,5},{5,4},{6,7},{7,6},{8,9},{9,8},{10,11... | collective-permute-start | bytes 786440 | tf_op jit(solution)/shard_map/ppermute | solution.py:209
  21.4 8.7 %collective-permute-start.12 = (f32[16,16,256]{2,1,0:T(8,128)S(1)}, f32[16,16,256]{2,1,0:T(8,128)S(1)}, u32[]{:S(2)}, u32[]{:S(2)}) collective-permute-start(f32[16,16,256]{2,1,0:T(8,128)S(1)} %pad_maximum_fusion.2), channel_id=1, source_target_pairs={{0,1},{1,0},{2,3},{3,2},{4,5},{5,4},{6,7},{7,6},{8,9},{9,8},{10,11... | collective-permute-start | bytes 786440 | tf_op jit(solution)/shard_map/ppermute | solution.py:209
  21.5 5.0 %collective-permute-start.8 = (f32[8,16,256]{2,1,0:T(8,128)S(1)}, f32[8,16,256]{2,1,0:T(8,128)S(1)}, u32[]{:S(2)}, u32[]{:S(2)}) collective-permute-start(f32[8,16,256]{2,1,0:T(8,128)S(1)} %collective-permute-done.6.refs_4_), channel_id=1, source_target_pairs={{0,2},{1,9},{2,0},{3,11},{4,6},{5,13},{6,4},{7,15},{8,10},{9,1},{1... | collective-permute-start | bytes 393224 | tf_op jit(solution)/shard_map/ppermute | solution.py:209
  24.5 5.6 %collective-permute-start.11 = (f32[16,16,256]{2,1,0:T(8,128)S(1)}, f32[16,16,256]{2,1,0:T(8,128)S(1)}, u32[]{:S(2)}, u32[]{:S(2)}) collective-permute-start(f32[16,16,256]{2,1,0:T(8,128)S(1)} %pad_maximum_fusion.1), channel_id=1, source_target_pairs={{0,1},{1,0},{2,3},{3,2},{4,5},{5,4},{6,7},{7,6},{8,9},{9,8},{10,11... | collective-permute-start | bytes 786440 | tf_op jit(solution)/shard_map/ppermute | solution.py:209
  24.6 5.0 %collective-permute-start.9 = (f32[8,16,256]{2,1,0:T(8,128)S(1)}, f32[8,16,256]{2,1,0:T(8,128)S(1)}, u32[]{:S(2)}, u32[]{:S(2)}) collective-permute-start(f32[8,16,256]{2,1,0:T(8,128)S(1)} %collective-permute-done.7.refs_5_), channel_id=1, source_target_pairs={{0,2},{1,9},{2,0},{3,11},{4,6},{5,13},{6,4},{7,15},{8,10},{9,1},{1... | collective-permute-start | bytes 393224 | tf_op jit(solution)/shard_map/ppermute | solution.py:209
  26.5 3.6 %collective-permute-start.13 = (f32[8,16,256]{2,1,0:T(8,128)S(1)}, f32[8,16,256]{2,1,0:T(8,128)S(1)}, u32[]{:S(2)}, u32[]{:S(2)}) collective-permute-start(f32[8,16,256]{2,1,0:T(8,128)S(1)} %collective-permute-done.8.refs_6_), channel_id=1, source_target_pairs={{0,1},{1,0},{2,3},{3,2},{4,5},{5,4},{6,7},{7,6},{8,9},{9,8},{10,11... | collective-permute-start | bytes 393224 | tf_op jit(solution)/shard_map/ppermute | solution.py:209
  29.6 1.5 %collective-permute-start.14 = (f32[8,16,256]{2,1,0:T(8,128)S(1)}, f32[8,16,256]{2,1,0:T(8,128)S(1)}, u32[]{:S(2)}, u32[]{:S(2)}) collective-permute-start(f32[8,16,256]{2,1,0:T(8,128)S(1)} %collective-permute-done.9.refs_7_), channel_id=1, source_target_pairs={{0,1},{1,0},{2,3},{3,2},{4,5},{5,4},{6,7},{7,6},{8,9},{9,8},{10,11... | collective-permute-start | bytes 393224 | tf_op jit(solution)/shard_map/ppermute | solution.py:209

commit v4 on v3

--- a/solution.py
+++ b/solution.py
@@ -37,6 +37,7 @@
         copy.wait()
     labels = lax.broadcasted_iota(jnp.int32, (clusters, slots), 0)
     position = lax.broadcasted_iota(jnp.int32, (top, slots), 1)
+    assigned = []
     for image in range(images):
         valid_ids = jnp.where(position < counts[image], ids[image], -1)
         values = weights[image].astype(F32)
@@ -46,9 +47,11 @@
             assign = assign + jnp.where(matched, values[slot : slot + 1], 0.0)
         assign = assign.astype(BF16)
         weight_sum = jnp.sum(assign.astype(F32), axis=1, keepdims=True)
-        large[image].wait()
-        residual = jnp.dot(assign, features[image], preferred_element_type=F32)
-        residual = residual - weight_sum * centroids[...].astype(F32)
+        assigned.append((assign, weight_sum * centroids[...].astype(F32)))
+    for copy in large:
+        copy.wait()
+    for image, (assign, offset) in enumerate(assigned):
+        residual = jnp.dot(assign, features[image], preferred_element_type=F32) - offset
         square = jnp.sum(residual * residual, axis=1, keepdims=True)
         rows[image] = residual / jnp.sqrt(square + 1e-06)
 
@@ -119,7 +122,7 @@
         start = slot * part
         return pieces[start // size][start % size : start % size + part, cluster, :]
 
-    def prepare(row_refs, col_refs, base):
+    def prepare_columns(col_refs, base):
         slots = [(j, t) for j in range(peers) for t in range(peers)]
         for k in range(half):
             pieces = [take(col_refs[t], j, base + k) for j, t in slots]
@@ -128,20 +131,26 @@
             right[0 * count : 1 * count, columns] = high
             right[1 * count : 2 * count, columns] = low
             right[2 * count : 3 * count, columns] = high
-        for k in range(block):
+
+    def prepare_rows(row_refs, clusters):
+        for k in clusters:
             pieces = [ref[:, k, :] for refs_of in row_refs for ref in refs_of]
             high, low = split(jnp.concatenate(pieces, axis=0))
             left[k, 0 * count : 1 * count] = high
             left[k, 1 * count : 2 * count] = high
             left[k, 2 * count : 3 * count] = low
 
+    lead = min(stages, block)
+
     @pl.when(core == 0)
     def _():
-        prepare(mine, theirs, 0)
+        prepare_columns(theirs, 0)
+        prepare_rows(mine, range(lead))
 
     @pl.when(core == 1)
     def _():
-        prepare(theirs, mine, half)
+        prepare_columns(mine, half)
+        prepare_rows(theirs, range(lead))
 
     def copy_out(step, slot):
         start = pl.multiple_of(step * width, width)
@@ -162,7 +171,17 @@
         copy_out(step, slot).start()
         return carry
 
-    lax.fori_loop(0, block, row_step, 0)
+    lax.fori_loop(0, lead, row_step, 0)
+
+    @pl.when(core == 0)
+    def _():
+        prepare_rows(mine, range(lead, block))
+
+    @pl.when(core == 1)
+    def _():
+        prepare_rows(theirs, range(lead, block))
+
+    lax.fori_loop(lead, block, row_step, 0)
     for step in range(max(block - stages, 0), block):
         copy_out(step, step % stages).wait()
 
@@ -228,9 +247,13 @@
     mine = [gathered]
     for k in range(1, peers):
         low = k & -k
+        pieces = [jnp.concatenate(gathered)] if k == 1 else gathered
         arrived = []
-        for piece in mine[k - low]:
-            arrived.append(second(piece, low))
+        for n, piece in enumerate(pieces):
+            if k != low and n == 0:
+                arrived.append(second(mine[k - low][n], low))
+            else:
+                arrived.append(second(piece, k))
         mine.append(arrived)
     theirs = []
     for k in range(peers):

time: 43.5 us -> 44.6 us (1.025)
  waiting for transfers between devices: 11 us -> 17.6 us
  starting transfers between devices: 16.8 us -> 12.2 us
  Pallas kernels: 15.4 us -> 14.5 us
    ppermute x15 -> x14, waiting for transfers between devices: 11 us -> 17.6 us  [send(): return lax.ppermute(value, ('img', 'tile'), pairs)]
    ppermute x15 -> x14, starting transfers between devices: 16.8 us -> 12.2 us  [send(): return lax.ppermute(value, ('img', 'tile'), pairs)]
  transfers between devices with their start and end apart: 15 -> 14, of which waited for: 8 -> 7; matrix products, arithmetic and copies ran while one was open for 0% -> 0% of each run, Pallas kernels for 0% -> 0%
where the time goes in v4:
time: 44.6 us; the launch traced here: 44.4 us
  waiting for transfers between devices  17.6 us (39%)
  Pallas kernels  14.5 us (33%)
  starting transfers between devices  12.2 us (27%)
    ppermute x14, waiting for transfers between devices, send(): return lax.ppermute(value, ('img', 'tile'), pairs)  17.6 us
    ppermute x14, starting transfers between devices, send(): return lax.ppermute(value, ('img', 'tile'), pairs)  12.2 us
    pallas_call x1, Pallas kernels, update(): pl.pallas_call(functools.partial(update_kernel, peers, factor, stages, si...  11.8 us
    pallas_call x1, Pallas kernels, aggregate(): pl.pallas_call(aggregate_kernel, in_specs=[pl.BlockSpec(memory_space=pltp...  2.75 us
  transfers between devices with their start and end apart: 14, of which 7 were waited for; matrix products, arithmetic and copies ran while one was open for 0% of the time, Pallas kernels for 0%

profile of v4, /device:TPU:0, one launch (start us, length us, event | category | flops | bytes accessed | tf_op | source)
XLA Modules:
  0.0 44.4 jit_solution(8301676645402648355)
XLA Ops:
  0.0 2.8 %aggregate.1.own = f32[2,64,256]{2,1,0:T(8,128)S(1)} custom-call(s32[2]{0:T(128)} %counts_in.1, s32[2,4,2400]{2,1,0:T(4,128)} %ids_in.1, bf16[2,4,2400]{2,1,0:T(4,128)(2,1)} %weights_in.1, bf16[64,256]{1,0:T(8,128)(2,1)} %centroids_in.1, bf16[2,2400,256]{2,1,0:T(8,128)(2,1)} %features_in.1), custom_call_target="tpu_custom_call" | custom-call | tf_op jit(solution)/shard_map/aggregate/pallas_call | solution.py:62
  2.8 0.0 copy-start
  2.8 0.6 %collective-permute-start = (f32[2,64,256]{2,1,0:T(8,128)S(1)}, f32[2,64,256]{2,1,0:T(8,128)S(1)}, u32[]{:S(2)}, u32[]{:S(2)}) collective-permute-start(f32[2,64,256]{2,1,0:T(8,128)S(1)} %aggregate.1.own), channel_id=1, source_target_pairs={{0,1},{1,0},{2,3},{3,2},{4,5},{5,4},{6,7},{7,6},{8,9},{9,8},{10,11... | collective-permute-start | bytes 393224 | tf_op jit(solution)/shard_map/ppermute | solution.py:228
  3.3 1.0 %collective-permute-done.other = f32[2,64,256]{2,1,0:T(8,128)S(1)} collective-permute-done((f32[2,64,256]{2,1,0:T(8,128)S(1)}, f32[2,64,256]{2,1,0:T(8,128)S(1)}, u32[]{:S(2)}, u32[]{:S(2)}) %collective-permute-start) | collective-permute-done | bytes 131104 | tf_op jit(solution)/shard_map/ppermute | solution.py:228
  4.3 3.0 %collective-permute-start.1 = (f32[4,16,256]{2,1,0:T(8,128)S(1)}, f32[4,16,256]{2,1,0:T(8,128)S(1)}, u32[]{:S(2)}, u32[]{:S(2)}) collective-permute-start(f32[4,16,256]{2,1,0:T(8,128)S(1)} %get-tuple-element.10), channel_id=1, source_target_pairs={{0,8},{1,3},{2,10},{3,1},{4,12},{5,7},{6,14},{7,5},{8,0},{9,11},{1... | collective-permute-start | bytes 196616 | tf_op jit(solution)/shard_map/ppermute | solution.py:228
  7.3 2.6 %collective-permute-start.2 = (f32[4,16,256]{2,1,0:T(8,128)S(1)}, f32[4,16,256]{2,1,0:T(8,128)S(1)}, u32[]{:S(2)}, u32[]{:S(2)}) collective-permute-start(f32[4,16,256]{2,1,0:T(8,128)S(1)} %get-tuple-element.11), channel_id=1, source_target_pairs={{0,16},{1,5},{2,18},{3,7},{4,20},{5,1},{6,22},{7,3},{8,24},{9,13},... | collective-permute-start | bytes 196616 | tf_op jit(solution)/shard_map/ppermute | solution.py:228
  9.9 0.0 collective-permute-start.3
  10.0 3.2 %collective-permute-done.2 = f32[4,16,256]{2,1,0:T(8,128)S(1)} collective-permute-done((f32[4,16,256]{2,1,0:T(8,128)S(1)}, f32[4,16,256]{2,1,0:T(8,128)S(1)}, u32[]{:S(2)}, u32[]{:S(2)}) %collective-permute-start.2) | collective-permute-done | bytes 65568 | tf_op jit(solution)/shard_map/ppermute | solution.py:228
  13.2 2.8 %collective-permute-done.3 = f32[4,16,256]{2,1,0:T(8,128)S(1)} collective-permute-done((f32[4,16,256]{2,1,0:T(8,128)S(1)}, f32[4,16,256]{2,1,0:T(8,128)S(1)}, u32[]{:S(2)}, u32[]{:S(2)}) %collective-permute-start.3) | collective-permute-done | bytes 65568 | tf_op jit(solution)/shard_map/ppermute | solution.py:228
  16.1 1.6 %collective-permute-start.4 = (f32[16,16,256]{2,1,0:T(8,128)S(1)}, f32[16,16,256]{2,1,0:T(8,128)S(1)}, u32[]{:S(2)}, u32[]{:S(2)}) collective-permute-start(f32[16,16,256]{2,1,0:T(8,128)S(1)} %get-tuple-element.13), channel_id=1, source_target_pairs={{0,2},{1,9},{2,0},{3,11},{4,6},{5,13},{6,4},{7,15},{8,10},{9,1},{1... | collective-permute-start | bytes 786440 | tf_op jit(solution)/shard_map/ppermute | solution.py:228
  17.7 2.2 %collective-permute-start.6 = (f32[8,16,256]{2,1,0:T(8,128)S(1)}, f32[8,16,256]{2,1,0:T(8,128)S(1)}, u32[]{:S(2)}, u32[]{:S(2)}) collective-permute-start(f32[8,16,256]{2,1,0:T(8,128)S(1)} %get-tuple-element.14.refs_1_), channel_id=1, source_target_pairs={{0,4},{1,17},{2,6},{3,19},{4,0},{5,21},{6,2},{7,23},{8,12},{9,25},... | collective-permute-start | bytes 393224 | tf_op jit(solution)/shard_map/ppermute | solution.py:228
  19.8 0.0 collective-permute-start.5
  19.9 1.5 %collective-permute-start.8 = (f32[8,16,256]{2,1,0:T(8,128)S(1)}, f32[8,16,256]{2,1,0:T(8,128)S(1)}, u32[]{:S(2)}, u32[]{:S(2)}) collective-permute-start(f32[8,16,256]{2,1,0:T(8,128)S(1)} %get-tuple-element.14.refs_1_), channel_id=1, source_target_pairs={{0,6},{1,25},{2,4},{3,27},{4,2},{5,29},{6,0},{7,31},{8,14},{9,17},... | collective-permute-start | bytes 393224 | tf_op jit(solution)/shard_map/ppermute | solution.py:228
  21.4 0.0 collective-permute-start.9
  21.4 1.4 %collective-permute-done.6.refs_4_ = f32[8,16,256]{2,1,0:T(8,128)S(1)} collective-permute-done((f32[8,16,256]{2,1,0:T(8,128)S(1)}, f32[8,16,256]{2,1,0:T(8,128)S(1)}, u32[]{:S(2)}, u32[]{:S(2)}) %collective-permute-start.6) | collective-permute-done | bytes 131104 | tf_op jit(solution)/shard_map/ppermute | solution.py:228
  22.8 3.4 %collective-permute-done.5.refs_3_ = f32[8,16,256]{2,1,0:T(8,128)S(1)} collective-permute-done((f32[8,16,256]{2,1,0:T(8,128)S(1)}, f32[8,16,256]{2,1,0:T(8,128)S(1)}, u32[]{:S(2)}, u32[]{:S(2)}) %collective-permute-start.5) | collective-permute-done | bytes 131104 | tf_op jit(solution)/shard_map/ppermute | solution.py:228
  26.2 0.1 collective-permute-start.11
  26.3 0.1 collective-permute-start.7
  26.4 0.4 collective-permute-start.10
  26.8 0.0 collective-permute-done.8.refs_6_
  26.8 0.2 collective-permute-start.13
  27.0 4.4 %collective-permute-done.7.refs_5_ = f32[8,16,256]{2,1,0:T(8,128)S(1)} collective-permute-done((f32[8,16,256]{2,1,0:T(8,128)S(1)}, f32[8,16,256]{2,1,0:T(8,128)S(1)}, u32[]{:S(2)}, u32[]{:S(2)}) %collective-permute-start.7) | collective-permute-done | bytes 131104 | tf_op jit(solution)/shard_map/ppermute | solution.py:228
  31.4 1.3 %collective-permute-done.12.refs_10_ = f32[8,16,256]{2,1,0:T(8,128)S(1)} collective-permute-done((f32[8,16,256]{2,1,0:T(8,128)S(1)}, f32[8,16,256]{2,1,0:T(8,128)S(1)}, u32[]{:S(2)}, u32[]{:S(2)}) %collective-permute-start.12) | collective-permute-done | bytes 131104 | tf_op jit(solution)/shard_map/ppermute | solution.py:228
  32.7 11.8 %update.1 = f32[4096,2048]{1,0:T(8,128)} custom-call(f32[8,16,256]{2,1,0:T(8,128)S(1)} %get-tuple-element.18.refs_0_, f32[8,16,256]{2,1,0:T(8,128)S(1)} %get-tuple-element.14.refs_1_, f32[16,16,256]{2,1,0:T(8,128)S(1)} %collective-permute-done.4.refs_2_, f32[8,16,256]{2,1,0:T(8,128)S(1)} %collective-permute-done.5.refs_3_, ...), custom_call_target="tpu_custom_call" | custom-call | tf_op jit(solution)/shard_map/update/pallas_call | solution.py:197
  (14 shorter events, 0.1 us)
Async XLA Ops:
  2.8 29.9 %copy-start = (f32[4096,2048]{1,0:T(8,128)S(1)}, f32[4096,2048]{1,0:T(8,128)}, u32[]{:S(2)}) copy-start(f32[4096,2048]{1,0:T(8,128)} %refs_12_.1) | copy-start | bytes 100663296
  2.8 1.5 %collective-permute-start = (f32[2,64,256]{2,1,0:T(8,128)S(1)}, f32[2,64,256]{2,1,0:T(8,128)S(1)}, u32[]{:S(2)}, u32[]{:S(2)}) collective-permute-start(f32[2,64,256]{2,1,0:T(8,128)S(1)} %aggregate.1.own), channel_id=1, source_target_pairs={{0,1},{1,0},{2,3},{3,2},{4,5},{5,4},{6,7},{7,6},{8,9},{9,8},{10,11... | collective-permute-start | bytes 393224 | tf_op jit(solution)/shard_map/ppermute | solution.py:228
  4.3 5.6 %collective-permute-start.1 = (f32[4,16,256]{2,1,0:T(8,128)S(1)}, f32[4,16,256]{2,1,0:T(8,128)S(1)}, u32[]{:S(2)}, u32[]{:S(2)}) collective-permute-start(f32[4,16,256]{2,1,0:T(8,128)S(1)} %get-tuple-element.10), channel_id=1, source_target_pairs={{0,8},{1,3},{2,10},{3,1},{4,12},{5,7},{6,14},{7,5},{8,0},{9,11},{1... | collective-permute-start | bytes 196616 | tf_op jit(solution)/shard_map/ppermute | solution.py:228
  7.3 5.9 %collective-permute-start.2 = (f32[4,16,256]{2,1,0:T(8,128)S(1)}, f32[4,16,256]{2,1,0:T(8,128)S(1)}, u32[]{:S(2)}, u32[]{:S(2)}) collective-permute-start(f32[4,16,256]{2,1,0:T(8,128)S(1)} %get-tuple-element.11), channel_id=1, source_target_pairs={{0,16},{1,5},{2,18},{3,7},{4,20},{5,1},{6,22},{7,3},{8,24},{9,13},... | collective-permute-start | bytes 196616 | tf_op jit(solution)/shard_map/ppermute | solution.py:228
  9.9 6.1 %collective-permute-start.3 = (f32[4,16,256]{2,1,0:T(8,128)S(1)}, f32[4,16,256]{2,1,0:T(8,128)S(1)}, u32[]{:S(2)}, u32[]{:S(2)}) collective-permute-start(f32[4,16,256]{2,1,0:T(8,128)S(1)} %get-tuple-element.12), channel_id=1, source_target_pairs={{0,24},{1,7},{2,26},{3,5},{4,28},{5,3},{6,30},{7,1},{8,16},{9,15},... | collective-permute-start | bytes 196616 | tf_op jit(solution)/shard_map/ppermute | solution.py:228
  16.1 10.3 %collective-permute-start.4 = (f32[16,16,256]{2,1,0:T(8,128)S(1)}, f32[16,16,256]{2,1,0:T(8,128)S(1)}, u32[]{:S(2)}, u32[]{:S(2)}) collective-permute-start(f32[16,16,256]{2,1,0:T(8,128)S(1)} %get-tuple-element.13), channel_id=1, source_target_pairs={{0,2},{1,9},{2,0},{3,11},{4,6},{5,13},{6,4},{7,15},{8,10},{9,1},{1... | collective-permute-start | bytes 786440 | tf_op jit(solution)/shard_map/ppermute | solution.py:228
  17.7 5.1 %collective-permute-start.6 = (f32[8,16,256]{2,1,0:T(8,128)S(1)}, f32[8,16,256]{2,1,0:T(8,128)S(1)}, u32[]{:S(2)}, u32[]{:S(2)}) collective-permute-start(f32[8,16,256]{2,1,0:T(8,128)S(1)} %get-tuple-element.14.refs_1_), channel_id=1, source_target_pairs={{0,4},{1,17},{2,6},{3,19},{4,0},{5,21},{6,2},{7,23},{8,12},{9,25},... | collective-permute-start | bytes 393224 | tf_op jit(solution)/shard_map/ppermute | solution.py:228
  19.8 6.4 %collective-permute-start.5 = (f32[8,16,256]{2,1,0:T(8,128)S(1)}, f32[8,16,256]{2,1,0:T(8,128)S(1)}, u32[]{:S(2)}, u32[]{:S(2)}) collective-permute-start(f32[8,16,256]{2,1,0:T(8,128)S(1)} %get-tuple-element.18.refs_0_), channel_id=1, source_target_pairs={{0,4},{1,17},{2,6},{3,19},{4,0},{5,21},{6,2},{7,23},{8,12},{9,25},... | collective-permute-start | bytes 393224 | tf_op jit(solution)/shard_map/ppermute | solution.py:228
  19.9 7.0 %collective-permute-start.8 = (f32[8,16,256]{2,1,0:T(8,128)S(1)}, f32[8,16,256]{2,1,0:T(8,128)S(1)}, u32[]{:S(2)}, u32[]{:S(2)}) collective-permute-start(f32[8,16,256]{2,1,0:T(8,128)S(1)} %get-tuple-element.14.refs_1_), channel_id=1, source_target_pairs={{0,6},{1,25},{2,4},{3,27},{4,2},{5,29},{6,0},{7,31},{8,14},{9,17},... | collective-permute-start | bytes 393224 | tf_op jit(solution)/shard_map/ppermute | solution.py:228
  21.4 10.0 %collective-permute-start.9 = (f32[16,16,256]{2,1,0:T(8,128)S(1)}, f32[16,16,256]{2,1,0:T(8,128)S(1)}, u32[]{:S(2)}, u32[]{:S(2)}) collective-permute-start(f32[16,16,256]{2,1,0:T(8,128)S(1)} %get-tuple-element.13), channel_id=1, source_target_pairs={{0,1},{1,0},{2,3},{3,2},{4,5},{5,4},{6,7},{7,6},{8,9},{9,8},{10,11... | collective-permute-start | bytes 786440 | tf_op jit(solution)/shard_map/ppermute | solution.py:228
  26.2 5.1 %collective-permute-start.11 = (f32[16,16,256]{2,1,0:T(8,128)S(1)}, f32[16,16,256]{2,1,0:T(8,128)S(1)}, u32[]{:S(2)}, u32[]{:S(2)}) collective-permute-start(f32[16,16,256]{2,1,0:T(8,128)S(1)} %pad_maximum_fusion), channel_id=1, source_target_pairs={{0,1},{1,0},{2,3},{3,2},{4,5},{5,4},{6,7},{7,6},{8,9},{9,8},{10,11... | collective-permute-start | bytes 786440 | tf_op jit(solution)/shard_map/ppermute | solution.py:228
  26.3 5.0 %collective-permute-start.7 = (f32[8,16,256]{2,1,0:T(8,128)S(1)}, f32[8,16,256]{2,1,0:T(8,128)S(1)}, u32[]{:S(2)}, u32[]{:S(2)}) collective-permute-start(f32[8,16,256]{2,1,0:T(8,128)S(1)} %collective-permute-done.5.refs_3_), channel_id=1, source_target_pairs={{0,2},{1,9},{2,0},{3,11},{4,6},{5,13},{6,4},{7,15},{8,10},{9,1},{1... | collective-permute-start | bytes 393224 | tf_op jit(solution)/shard_map/ppermute | solution.py:228
  26.4 6.3 %collective-permute-start.10 = (f32[16,16,256]{2,1,0:T(8,128)S(1)}, f32[16,16,256]{2,1,0:T(8,128)S(1)}, u32[]{:S(2)}, u32[]{:S(2)}) collective-permute-start(f32[16,16,256]{2,1,0:T(8,128)S(1)} %collective-permute-done.4.refs_2_), channel_id=1, source_target_pairs={{0,1},{1,0},{2,3},{3,2},{4,5},{5,4},{6,7},{7,6},{8,9},{9,8},{10,11... | collective-permute-start | bytes 786440 | tf_op jit(solution)/shard_map/ppermute | solution.py:228
  26.8 4.5 %collective-permute-start.13 = (f32[8,16,256]{2,1,0:T(8,128)S(1)}, f32[8,16,256]{2,1,0:T(8,128)S(1)}, u32[]{:S(2)}, u32[]{:S(2)}) collective-permute-start(f32[8,16,256]{2,1,0:T(8,128)S(1)} %collective-permute-done.8.refs_6_), channel_id=1, source_target_pairs={{0,1},{1,0},{2,3},{3,2},{4,5},{5,4},{6,7},{7,6},{8,9},{9,8},{10,11... | collective-permute-start | bytes 393224 | tf_op jit(solution)/shard_map/ppermute | solution.py:228
  31.3 1.3 %collective-permute-start.12 = (f32[8,16,256]{2,1,0:T(8,128)S(1)}, f32[8,16,256]{2,1,0:T(8,128)S(1)}, u32[]{:S(2)}, u32[]{:S(2)}) collective-permute-start(f32[8,16,256]{2,1,0:T(8,128)S(1)} %collective-permute-done.7.refs_5_), channel_id=1, source_target_pairs={{0,1},{1,0},{2,3},{3,2},{4,5},{5,4},{6,7},{7,6},{8,9},{9,8},{10,11... | collective-permute-start | bytes 393224 | tf_op jit(solution)/shard_map/ppermute | solution.py:228

commit v5 on v4

--- a/solution.py
+++ b/solution.py
@@ -140,7 +140,7 @@
             left[k, 1 * count : 2 * count] = high
             left[k, 2 * count : 3 * count] = low
 
-    lead = min(stages, block)
+    lead = min(2, block)
 
     @pl.when(core == 0)
     def _():
@@ -193,7 +193,7 @@
     block, width = flat[0].shape[1:]
     count = sum(piece.shape[0] for pieces in mine for piece in pieces)
     rows, cols = covariance.shape
-    stages = 3
+    stages = 4
     return pl.pallas_call(
         functools.partial(update_kernel, peers, factor, stages, sizes),
         in_specs=[pl.BlockSpec(memory_space=VMEM)] * (len(flat) + 1),
@@ -205,7 +205,7 @@
             VMEM((stages, width, cols), F32),
             pltpu.SemaphoreType.DMA((stages,)),
         ],
-        compiler_params=pltpu.CompilerParams(vmem_limit_bytes=12 << 20),
+        compiler_params=pltpu.CompilerParams(vmem_limit_bytes=14 << 20),
         name="update",
     )(*flat, covariance)
 

time: 44.6 us -> 44.6 us (level)
  no operation moved by 1% of the time
where the time goes in v5:
time: 44.6 us; the launch traced here: 44.4 us
  waiting for transfers between devices  17.6 us (39%)
  Pallas kernels  14.5 us (33%)
  starting transfers between devices  12.2 us (27%)
    ppermute x14, waiting for transfers between devices, send(): return lax.ppermute(value, ('img', 'tile'), pairs)  17.6 us
    ppermute x14, starting transfers between devices, send(): return lax.ppermute(value, ('img', 'tile'), pairs)  12.2 us
    pallas_call x1, Pallas kernels, update(): pl.pallas_call(functools.partial(update_kernel, peers, factor, stages, si...  11.7 us
    pallas_call x1, Pallas kernels, aggregate(): pl.pallas_call(aggregate_kernel, in_specs=[pl.BlockSpec(memory_space=pltp...  2.75 us
  transfers between devices with their start and end apart: 14, of which 7 were waited for; matrix products, arithmetic and copies ran while one was open for 0% of the time, Pallas kernels for 0%

profile of v5, /device:TPU:0, one launch (start us, length us, event | category | flops | bytes accessed | tf_op | source)
XLA Modules:
  0.0 44.4 jit_solution(17132190371931084084)
XLA Ops:
  0.0 2.8 %aggregate.1.own = f32[2,64,256]{2,1,0:T(8,128)S(1)} custom-call(s32[2]{0:T(128)} %counts_in.1, s32[2,4,2400]{2,1,0:T(4,128)} %ids_in.1, bf16[2,4,2400]{2,1,0:T(4,128)(2,1)} %weights_in.1, bf16[64,256]{1,0:T(8,128)(2,1)} %centroids_in.1, bf16[2,2400,256]{2,1,0:T(8,128)(2,1)} %features_in.1), custom_call_target="tpu_custom_call" | custom-call | tf_op jit(solution)/shard_map/aggregate/pallas_call | solution.py:62
  2.8 0.0 copy-start
  2.8 0.6 %collective-permute-start = (f32[2,64,256]{2,1,0:T(8,128)S(1)}, f32[2,64,256]{2,1,0:T(8,128)S(1)}, u32[]{:S(2)}, u32[]{:S(2)}) collective-permute-start(f32[2,64,256]{2,1,0:T(8,128)S(1)} %aggregate.1.own), channel_id=1, source_target_pairs={{0,1},{1,0},{2,3},{3,2},{4,5},{5,4},{6,7},{7,6},{8,9},{9,8},{10,11... | collective-permute-start | bytes 393224 | tf_op jit(solution)/shard_map/ppermute | solution.py:228
  3.3 1.0 %collective-permute-done.other = f32[2,64,256]{2,1,0:T(8,128)S(1)} collective-permute-done((f32[2,64,256]{2,1,0:T(8,128)S(1)}, f32[2,64,256]{2,1,0:T(8,128)S(1)}, u32[]{:S(2)}, u32[]{:S(2)}) %collective-permute-start) | collective-permute-done | bytes 131104 | tf_op jit(solution)/shard_map/ppermute | solution.py:228
  4.3 3.0 %collective-permute-start.1 = (f32[4,16,256]{2,1,0:T(8,128)S(1)}, f32[4,16,256]{2,1,0:T(8,128)S(1)}, u32[]{:S(2)}, u32[]{:S(2)}) collective-permute-start(f32[4,16,256]{2,1,0:T(8,128)S(1)} %get-tuple-element.10), channel_id=1, source_target_pairs={{0,8},{1,3},{2,10},{3,1},{4,12},{5,7},{6,14},{7,5},{8,0},{9,11},{1... | collective-permute-start | bytes 196616 | tf_op jit(solution)/shard_map/ppermute | solution.py:228
  7.3 2.6 %collective-permute-start.2 = (f32[4,16,256]{2,1,0:T(8,128)S(1)}, f32[4,16,256]{2,1,0:T(8,128)S(1)}, u32[]{:S(2)}, u32[]{:S(2)}) collective-permute-start(f32[4,16,256]{2,1,0:T(8,128)S(1)} %get-tuple-element.11), channel_id=1, source_target_pairs={{0,16},{1,5},{2,18},{3,7},{4,20},{5,1},{6,22},{7,3},{8,24},{9,13},... | collective-permute-start | bytes 196616 | tf_op jit(solution)/shard_map/ppermute | solution.py:228
  9.9 0.0 collective-permute-start.3
  10.0 3.2 %collective-permute-done.2 = f32[4,16,256]{2,1,0:T(8,128)S(1)} collective-permute-done((f32[4,16,256]{2,1,0:T(8,128)S(1)}, f32[4,16,256]{2,1,0:T(8,128)S(1)}, u32[]{:S(2)}, u32[]{:S(2)}) %collective-permute-start.2) | collective-permute-done | bytes 65568 | tf_op jit(solution)/shard_map/ppermute | solution.py:228
  13.2 2.8 %collective-permute-done.3 = f32[4,16,256]{2,1,0:T(8,128)S(1)} collective-permute-done((f32[4,16,256]{2,1,0:T(8,128)S(1)}, f32[4,16,256]{2,1,0:T(8,128)S(1)}, u32[]{:S(2)}, u32[]{:S(2)}) %collective-permute-start.3) | collective-permute-done | bytes 65568 | tf_op jit(solution)/shard_map/ppermute | solution.py:228
  16.1 1.6 %collective-permute-start.4 = (f32[16,16,256]{2,1,0:T(8,128)S(1)}, f32[16,16,256]{2,1,0:T(8,128)S(1)}, u32[]{:S(2)}, u32[]{:S(2)}) collective-permute-start(f32[16,16,256]{2,1,0:T(8,128)S(1)} %get-tuple-element.13), channel_id=1, source_target_pairs={{0,2},{1,9},{2,0},{3,11},{4,6},{5,13},{6,4},{7,15},{8,10},{9,1},{1... | collective-permute-start | bytes 786440 | tf_op jit(solution)/shard_map/ppermute | solution.py:228
  17.7 2.2 %collective-permute-start.6 = (f32[8,16,256]{2,1,0:T(8,128)S(1)}, f32[8,16,256]{2,1,0:T(8,128)S(1)}, u32[]{:S(2)}, u32[]{:S(2)}) collective-permute-start(f32[8,16,256]{2,1,0:T(8,128)S(1)} %get-tuple-element.14.refs_1_), channel_id=1, source_target_pairs={{0,4},{1,17},{2,6},{3,19},{4,0},{5,21},{6,2},{7,23},{8,12},{9,25},... | collective-permute-start | bytes 393224 | tf_op jit(solution)/shard_map/ppermute | solution.py:228
  19.8 0.0 collective-permute-start.5
  19.9 1.5 %collective-permute-start.8 = (f32[8,16,256]{2,1,0:T(8,128)S(1)}, f32[8,16,256]{2,1,0:T(8,128)S(1)}, u32[]{:S(2)}, u32[]{:S(2)}) collective-permute-start(f32[8,16,256]{2,1,0:T(8,128)S(1)} %get-tuple-element.14.refs_1_), channel_id=1, source_target_pairs={{0,6},{1,25},{2,4},{3,27},{4,2},{5,29},{6,0},{7,31},{8,14},{9,17},... | collective-permute-start | bytes 393224 | tf_op jit(solution)/shard_map/ppermute | solution.py:228
  21.4 0.0 collective-permute-start.9
  21.4 1.4 %collective-permute-done.6.refs_4_ = f32[8,16,256]{2,1,0:T(8,128)S(1)} collective-permute-done((f32[8,16,256]{2,1,0:T(8,128)S(1)}, f32[8,16,256]{2,1,0:T(8,128)S(1)}, u32[]{:S(2)}, u32[]{:S(2)}) %collective-permute-start.6) | collective-permute-done | bytes 131104 | tf_op jit(solution)/shard_map/ppermute | solution.py:228
  22.8 3.4 %collective-permute-done.5.refs_3_ = f32[8,16,256]{2,1,0:T(8,128)S(1)} collective-permute-done((f32[8,16,256]{2,1,0:T(8,128)S(1)}, f32[8,16,256]{2,1,0:T(8,128)S(1)}, u32[]{:S(2)}, u32[]{:S(2)}) %collective-permute-start.5) | collective-permute-done | bytes 131104 | tf_op jit(solution)/shard_map/ppermute | solution.py:228
  26.2 0.1 collective-permute-start.11
  26.3 0.1 collective-permute-start.7
  26.4 0.4 collective-permute-start.10
  26.8 0.0 collective-permute-done.8.refs_6_
  26.8 0.2 collective-permute-start.13
  27.0 4.4 %collective-permute-done.7.refs_5_ = f32[8,16,256]{2,1,0:T(8,128)S(1)} collective-permute-done((f32[8,16,256]{2,1,0:T(8,128)S(1)}, f32[8,16,256]{2,1,0:T(8,128)S(1)}, u32[]{:S(2)}, u32[]{:S(2)}) %collective-permute-start.7) | collective-permute-done | bytes 131104 | tf_op jit(solution)/shard_map/ppermute | solution.py:228
  31.4 1.3 %collective-permute-done.12.refs_10_ = f32[8,16,256]{2,1,0:T(8,128)S(1)} collective-permute-done((f32[8,16,256]{2,1,0:T(8,128)S(1)}, f32[8,16,256]{2,1,0:T(8,128)S(1)}, u32[]{:S(2)}, u32[]{:S(2)}) %collective-permute-start.12) | collective-permute-done | bytes 131104 | tf_op jit(solution)/shard_map/ppermute | solution.py:228
  32.7 11.7 %update.1 = f32[4096,2048]{1,0:T(8,128)} custom-call(f32[8,16,256]{2,1,0:T(8,128)S(1)} %get-tuple-element.18.refs_0_, f32[8,16,256]{2,1,0:T(8,128)S(1)} %get-tuple-element.14.refs_1_, f32[16,16,256]{2,1,0:T(8,128)S(1)} %collective-permute-done.4.refs_2_, f32[8,16,256]{2,1,0:T(8,128)S(1)} %collective-permute-done.5.refs_3_, ...), custom_call_target="tpu_custom_call" | custom-call | tf_op jit(solution)/shard_map/update/pallas_call | solution.py:197
  (14 shorter events, 0.1 us)
Async XLA Ops:
  2.8 29.9 %copy-start = (f32[4096,2048]{1,0:T(8,128)S(1)}, f32[4096,2048]{1,0:T(8,128)}, u32[]{:S(2)}) copy-start(f32[4096,2048]{1,0:T(8,128)} %refs_12_.1) | copy-start | bytes 100663296
  2.8 1.5 %collective-permute-start = (f32[2,64,256]{2,1,0:T(8,128)S(1)}, f32[2,64,256]{2,1,0:T(8,128)S(1)}, u32[]{:S(2)}, u32[]{:S(2)}) collective-permute-start(f32[2,64,256]{2,1,0:T(8,128)S(1)} %aggregate.1.own), channel_id=1, source_target_pairs={{0,1},{1,0},{2,3},{3,2},{4,5},{5,4},{6,7},{7,6},{8,9},{9,8},{10,11... | collective-permute-start | bytes 393224 | tf_op jit(solution)/shard_map/ppermute | solution.py:228
  4.3 5.6 %collective-permute-start.1 = (f32[4,16,256]{2,1,0:T(8,128)S(1)}, f32[4,16,256]{2,1,0:T(8,128)S(1)}, u32[]{:S(2)}, u32[]{:S(2)}) collective-permute-start(f32[4,16,256]{2,1,0:T(8,128)S(1)} %get-tuple-element.10), channel_id=1, source_target_pairs={{0,8},{1,3},{2,10},{3,1},{4,12},{5,7},{6,14},{7,5},{8,0},{9,11},{1... | collective-permute-start | bytes 196616 | tf_op jit(solution)/shard_map/ppermute | solution.py:228
  7.3 5.9 %collective-permute-start.2 = (f32[4,16,256]{2,1,0:T(8,128)S(1)}, f32[4,16,256]{2,1,0:T(8,128)S(1)}, u32[]{:S(2)}, u32[]{:S(2)}) collective-permute-start(f32[4,16,256]{2,1,0:T(8,128)S(1)} %get-tuple-element.11), channel_id=1, source_target_pairs={{0,16},{1,5},{2,18},{3,7},{4,20},{5,1},{6,22},{7,3},{8,24},{9,13},... | collective-permute-start | bytes 196616 | tf_op jit(solution)/shard_map/ppermute | solution.py:228
  9.9 6.1 %collective-permute-start.3 = (f32[4,16,256]{2,1,0:T(8,128)S(1)}, f32[4,16,256]{2,1,0:T(8,128)S(1)}, u32[]{:S(2)}, u32[]{:S(2)}) collective-permute-start(f32[4,16,256]{2,1,0:T(8,128)S(1)} %get-tuple-element.12), channel_id=1, source_target_pairs={{0,24},{1,7},{2,26},{3,5},{4,28},{5,3},{6,30},{7,1},{8,16},{9,15},... | collective-permute-start | bytes 196616 | tf_op jit(solution)/shard_map/ppermute | solution.py:228
  16.1 10.3 %collective-permute-start.4 = (f32[16,16,256]{2,1,0:T(8,128)S(1)}, f32[16,16,256]{2,1,0:T(8,128)S(1)}, u32[]{:S(2)}, u32[]{:S(2)}) collective-permute-start(f32[16,16,256]{2,1,0:T(8,128)S(1)} %get-tuple-element.13), channel_id=1, source_target_pairs={{0,2},{1,9},{2,0},{3,11},{4,6},{5,13},{6,4},{7,15},{8,10},{9,1},{1... | collective-permute-start | bytes 786440 | tf_op jit(solution)/shard_map/ppermute | solution.py:228
  17.7 5.1 %collective-permute-start.6 = (f32[8,16,256]{2,1,0:T(8,128)S(1)}, f32[8,16,256]{2,1,0:T(8,128)S(1)}, u32[]{:S(2)}, u32[]{:S(2)}) collective-permute-start(f32[8,16,256]{2,1,0:T(8,128)S(1)} %get-tuple-element.14.refs_1_), channel_id=1, source_target_pairs={{0,4},{1,17},{2,6},{3,19},{4,0},{5,21},{6,2},{7,23},{8,12},{9,25},... | collective-permute-start | bytes 393224 | tf_op jit(solution)/shard_map/ppermute | solution.py:228
  19.8 6.4 %collective-permute-start.5 = (f32[8,16,256]{2,1,0:T(8,128)S(1)}, f32[8,16,256]{2,1,0:T(8,128)S(1)}, u32[]{:S(2)}, u32[]{:S(2)}) collective-permute-start(f32[8,16,256]{2,1,0:T(8,128)S(1)} %get-tuple-element.18.refs_0_), channel_id=1, source_target_pairs={{0,4},{1,17},{2,6},{3,19},{4,0},{5,21},{6,2},{7,23},{8,12},{9,25},... | collective-permute-start | bytes 393224 | tf_op jit(solution)/shard_map/ppermute | solution.py:228
  19.9 7.0 %collective-permute-start.8 = (f32[8,16,256]{2,1,0:T(8,128)S(1)}, f32[8,16,256]{2,1,0:T(8,128)S(1)}, u32[]{:S(2)}, u32[]{:S(2)}) collective-permute-start(f32[8,16,256]{2,1,0:T(8,128)S(1)} %get-tuple-element.14.refs_1_), channel_id=1, source_target_pairs={{0,6},{1,25},{2,4},{3,27},{4,2},{5,29},{6,0},{7,31},{8,14},{9,17},... | collective-permute-start | bytes 393224 | tf_op jit(solution)/shard_map/ppermute | solution.py:228
  21.4 10.0 %collective-permute-start.9 = (f32[16,16,256]{2,1,0:T(8,128)S(1)}, f32[16,16,256]{2,1,0:T(8,128)S(1)}, u32[]{:S(2)}, u32[]{:S(2)}) collective-permute-start(f32[16,16,256]{2,1,0:T(8,128)S(1)} %get-tuple-element.13), channel_id=1, source_target_pairs={{0,1},{1,0},{2,3},{3,2},{4,5},{5,4},{6,7},{7,6},{8,9},{9,8},{10,11... | collective-permute-start | bytes 786440 | tf_op jit(solution)/shard_map/ppermute | solution.py:228
  26.2 5.1 %collective-permute-start.11 = (f32[16,16,256]{2,1,0:T(8,128)S(1)}, f32[16,16,256]{2,1,0:T(8,128)S(1)}, u32[]{:S(2)}, u32[]{:S(2)}) collective-permute-start(f32[16,16,256]{2,1,0:T(8,128)S(1)} %pad_maximum_fusion), channel_id=1, source_target_pairs={{0,1},{1,0},{2,3},{3,2},{4,5},{5,4},{6,7},{7,6},{8,9},{9,8},{10,11... | collective-permute-start | bytes 786440 | tf_op jit(solution)/shard_map/ppermute | solution.py:228
  26.3 5.0 %collective-permute-start.7 = (f32[8,16,256]{2,1,0:T(8,128)S(1)}, f32[8,16,256]{2,1,0:T(8,128)S(1)}, u32[]{:S(2)}, u32[]{:S(2)}) collective-permute-start(f32[8,16,256]{2,1,0:T(8,128)S(1)} %collective-permute-done.5.refs_3_), channel_id=1, source_target_pairs={{0,2},{1,9},{2,0},{3,11},{4,6},{5,13},{6,4},{7,15},{8,10},{9,1},{1... | collective-permute-start | bytes 393224 | tf_op jit(solution)/shard_map/ppermute | solution.py:228
  26.4 6.3 %collective-permute-start.10 = (f32[16,16,256]{2,1,0:T(8,128)S(1)}, f32[16,16,256]{2,1,0:T(8,128)S(1)}, u32[]{:S(2)}, u32[]{:S(2)}) collective-permute-start(f32[16,16,256]{2,1,0:T(8,128)S(1)} %collective-permute-done.4.refs_2_), channel_id=1, source_target_pairs={{0,1},{1,0},{2,3},{3,2},{4,5},{5,4},{6,7},{7,6},{8,9},{9,8},{10,11... | collective-permute-start | bytes 786440 | tf_op jit(solution)/shard_map/ppermute | solution.py:228
  26.8 4.5 %collective-permute-start.13 = (f32[8,16,256]{2,1,0:T(8,128)S(1)}, f32[8,16,256]{2,1,0:T(8,128)S(1)}, u32[]{:S(2)}, u32[]{:S(2)}) collective-permute-start(f32[8,16,256]{2,1,0:T(8,128)S(1)} %collective-permute-done.8.refs_6_), channel_id=1, source_target_pairs={{0,1},{1,0},{2,3},{3,2},{4,5},{5,4},{6,7},{7,6},{8,9},{9,8},{10,11... | collective-permute-start | bytes 393224 | tf_op jit(solution)/shard_map/ppermute | solution.py:228
  31.3 1.3 %collective-permute-start.12 = (f32[8,16,256]{2,1,0:T(8,128)S(1)}, f32[8,16,256]{2,1,0:T(8,128)S(1)}, u32[]{:S(2)}, u32[]{:S(2)}) collective-permute-start(f32[8,16,256]{2,1,0:T(8,128)S(1)} %collective-permute-done.7.refs_5_), channel_id=1, source_target_pairs={{0,1},{1,0},{2,3},{3,2},{4,5},{5,4},{6,7},{7,6},{8,9},{9,8},{10,11... | collective-permute-start | bytes 393224 | tf_op jit(solution)/shard_map/ppermute | solution.py:228
